TPU v7x, 32 devices: a whole 2x2x4 slice. The times are simulated.
32 devices in a mesh: dp: 4 (over y, x), row: 4 (over z), col: 2 (over core).
Axes of the slice: x: 2, y: 2, z: 4, core: 2. Of those that a mesh axis runs over, the one named last changes fastest.
Arguments:
- images: bfloat16 [32, 577, 1024], P(('dp', 'row'), None, 'col'), may hold values from -6 to 6
- cotangent: bfloat16 [32, 577, 1024], P(('dp', 'row'), None, 'col'), may hold values from -6 to 6
- micro_batch: int32 [32], P(('dp', 'row')), may hold values from 0 to 1, as said below
- heads_weight: bfloat16 [1024, 3, 1024], P('row', None, 'col'), may hold values from -0.1875 to 0.1875
- heads_bias: bfloat16 [2, 1024], P(None, 'col'), may hold values from -3 to 3
- merge_weight: bfloat16 [1024, 1024], P('col', 'row'), may hold values from -2 to 2
- merge_bias: bfloat16 [1024], P('col'), may hold values from -3 to 3
- expand_weight: bfloat16 [1024, 4096], P('row', 'col'), may hold values from -0.1875 to 0.1875
- expand_bias: bfloat16 [4096], P('col'), may hold values from -3 to 3
- shrink_weight: bfloat16 [4096, 1024], P('col', 'row'), may hold values from -0.09375 to 0.09375
- shrink_bias: bfloat16 [1024], P('col'), may hold values from -3 to 3
- norm_gains: bfloat16 [2, 1024], P(None, 'col'), may hold values from 0.5 to 1.5
- norm_shifts: bfloat16 [2, 1024], P(None, 'col'), may hold values from -2 to 2
Outputs:
- block_out: bfloat16 [32, 577, 1024], P(('dp', 'row'), None, 'col')
- input_grad: float32 [32, 577, 1024], P(('dp', 'row'), None, 'col')
- heads_weight_grad: float32 [1024, 3, 1024], P('row', None, 'col')
- heads_bias_grad: float32 [2, 1024], P(None, 'col')
- merge_weight_grad: float32 [1024, 1024], P('col', 'row')
- merge_bias_grad: float32 [1024], P('col')
- expand_weight_grad: float32 [1024, 4096], P('row', 'col')
- expand_bias_grad: float32 [4096], P('col')
- shrink_weight_grad: float32 [4096, 1024], P('col', 'row')
- shrink_bias_grad: float32 [1024], P('col')
- norm_gains_grad: float32 [2, 1024], P(None, 'col')
- norm_shifts_grad: float32 [2, 1024], P(None, 'col')
Inputs may be any that keep to these rules, and one draw needn't show every extreme that they name: `micro_batch`: every micro-batch number 0 to 1 belongs to at least one image.
All inputs are finite; a program needn't handle non-finite values.
Results may differ from a plain program's by a relative error of at most 0.018.
Values may be sent and summed in bfloat16 or wider, within the bound.
No kernel may reach another device: no remote copies, remote signals or barrier semaphores. Data moves between devices by JAX's collectives and lax.ppermute only.
A program may use at most 192 MiB of HBM per device.

v0:
```python
import jax
import jax.numpy as jnp
from jax import lax
from jax.sharding import PartitionSpec as P

HEAD_DIM = 64
MICRO = 2


def merged(value, axis, join):
    pieces = jax.tree.map(lambda part: lax.all_gather(part, axis), value)
    head = jax.tree.map(lambda part: part[0], pieces)
    tail = jax.tree.map(lambda part: part[1:], pieces)
    subtotal, _ = lax.scan(lambda subtotal, share: (join(subtotal, share), None), head, tail)
    return subtotal


def moments_join(first, second):
    count_sum = first[0] + second[0]
    offset = second[1] - first[1]
    joined_mean = first[1] + offset * (second[0] / count_sum)
    joined_spread = first[2] + second[2] + offset * offset * (first[0] * second[0] / count_sum)
    return (count_sum, joined_mean, joined_spread)


def norm_split(values, gain, shift, full_width):
    local_mean = jnp.mean(values, axis=1)
    local_spread = jnp.sum(jnp.square(values - local_mean[:, None]), axis=1)
    local_count = jnp.full(local_mean.shape, values.shape[1], jnp.float32)
    merged_count, row_mean, row_spread = merged(
        (local_count, local_mean, local_spread), "col", moments_join
    )
    inverse = lax.rsqrt(row_spread / full_width + 1e-05)
    centered = (values - row_mean[:, None]) * inverse[:, None]
    normed = (centered * gain + shift).astype(jnp.bfloat16)
    return (lax.all_gather(normed, "col", axis=1, tiled=True), centered, inverse)


def norm_back_split(partial_rows, centered, inverse, gain, full_width):
    summed = lax.psum_scatter(
        partial_rows.astype(jnp.bfloat16), "col", scatter_dimension=1, tiled=True
    ).astype(jnp.float32)
    scaled = summed * gain
    first_total, second_total = lax.psum(
        (jnp.sum(scaled, axis=1), jnp.sum(scaled * centered, axis=1)), "col"
    )
    result = inverse[:, None] * (
        scaled - first_total[:, None] / full_width - centered * (second_total[:, None] / full_width)
    )
    return (result, jnp.sum(summed * centered, axis=0), jnp.sum(summed, axis=0))


def gather_grads(values):
    return lax.all_gather(values, "col", axis=1, tiled=True)


def branch_split(partial_rows):
    return lax.psum_scatter(
        partial_rows.astype(jnp.bfloat16), "col", scatter_dimension=1, tiled=True
    ).astype(jnp.float32)


def attend(query_low, key_low, value_low):
    scores = jnp.einsum("qhe,khe->hqk", query_low, key_low, preferred_element_type=jnp.float32)
    log_total = jax.nn.logsumexp(scores, axis=-1)
    probabilities = jnp.exp(scores - log_total[..., None]).astype(jnp.bfloat16)
    attended = jnp.einsum(
        "hqk,khe->qhe", probabilities, value_low, preferred_element_type=jnp.float32
    )
    return (attended, log_total)


def attend_back(query_low, key_low, value_low, log_total, upstream):
    scores = jnp.einsum("qhe,khe->hqk", query_low, key_low, preferred_element_type=jnp.float32)
    probabilities = jnp.exp(scores - log_total[..., None])
    probs_low = probabilities.astype(jnp.bfloat16)
    value_grad = jnp.einsum(
        "hqk,qhe->khe", probs_low, upstream, preferred_element_type=jnp.float32
    ).astype(jnp.bfloat16)
    prob_grad = jnp.einsum("qhe,khe->hqk", upstream, value_low, preferred_element_type=jnp.float32)
    score_grad = (
        probabilities * (prob_grad - jnp.sum(prob_grad * probabilities, axis=-1, keepdims=True))
    ).astype(jnp.bfloat16)
    query_grad = jnp.einsum(
        "hqk,khe->qhe", score_grad, key_low, preferred_element_type=jnp.float32
    ).astype(jnp.bfloat16)
    key_grad = jnp.einsum(
        "hqk,qhe->khe", score_grad, query_low, preferred_element_type=jnp.float32
    ).astype(jnp.bfloat16)
    return (query_grad, key_grad, value_grad)


def own_slice(values, col_start, local_width):
    return lax.dynamic_slice_in_dim(values, col_start, local_width, 1)


def shards(
    images,
    cotangent,
    micro_batch,
    heads_weight,
    heads_bias,
    merge_weight,
    merge_bias,
    expand_weight,
    expand_bias,
    shrink_weight,
    shrink_bias,
    norm_gains,
    norm_shifts,
):
    local_width = images.shape[2]
    full_width = local_width * lax.axis_size("col")
    col_start = lax.axis_index("col") * local_width
    local_heads = local_width // HEAD_DIM
    length = images.shape[1]
    slot_count = images.shape[0]
    heads_full, merge_full, expand_full, shrink_full = (
        lax.all_gather(heads_weight, "row", axis=0, tiled=True),
        lax.all_gather(merge_weight, "row", axis=1, tiled=True),
        lax.all_gather(expand_weight, "row", axis=0, tiled=True),
        lax.all_gather(shrink_weight, "row", axis=1, tiled=True),
    )
    member = (micro_batch[:, None] == jnp.arange(MICRO, dtype=jnp.int32)[None, :]).astype(jnp.int32)
    totals = lax.psum(jnp.sum(member, axis=0), ("dp", "row"))
    all_slots = slot_count * lax.axis_size("dp") * lax.axis_size("row")
    batch_weight = all_slots / (MICRO * totals.astype(jnp.float32))
    slot_weight = jnp.sum(member.astype(jnp.float32) * batch_weight[None, :], axis=1)
    gains_own = norm_gains.astype(jnp.float32)
    shifts_own = norm_shifts.astype(jnp.float32)
    heads_bias_own = heads_bias.astype(jnp.float32)
    merge_bias_own = merge_bias.astype(jnp.float32)
    expand_bias_own = expand_bias.astype(jnp.float32)
    shrink_bias_own = shrink_bias.astype(jnp.float32)
    heads_grad = jnp.zeros(heads_full.shape, jnp.float32)
    merge_grad = jnp.zeros(merge_full.shape, jnp.float32)
    expand_grad = jnp.zeros(expand_full.shape, jnp.float32)
    shrink_grad = jnp.zeros(shrink_full.shape, jnp.float32)
    heads_bias_grad = jnp.zeros(heads_bias.shape, jnp.float32)
    merge_bias_grad = jnp.zeros(merge_bias.shape, jnp.float32)
    expand_bias_grad = jnp.zeros(expand_bias.shape, jnp.float32)
    shrink_bias_grad = jnp.zeros(shrink_bias.shape, jnp.float32)
    gain_grad = jnp.zeros(norm_gains.shape, jnp.float32)
    shift_grad = jnp.zeros(norm_shifts.shape, jnp.float32)
    outputs = []
    input_grads = []
    for slot_index in range(slot_count):
        own_input = images[slot_index].astype(jnp.float32)
        weight_now = slot_weight[slot_index]
        normed, centered_one, inverse_one = norm_split(
            own_input, gains_own[0], shifts_own[0], full_width
        )
        mixed_heads = jnp.einsum(
            "td,dkf->tkf", normed, heads_full, preferred_element_type=jnp.float32
        )
        query_low = (
            ((mixed_heads[:, 0] + heads_bias_own[0]) * HEAD_DIM ** (-0.5))
            .astype(jnp.bfloat16)
            .reshape(length, local_heads, HEAD_DIM)
        )
        key_low = mixed_heads[:, 1].astype(jnp.bfloat16).reshape(length, local_heads, HEAD_DIM)
        value_low = (
            (mixed_heads[:, 2] + heads_bias_own[1])
            .astype(jnp.bfloat16)
            .reshape(length, local_heads, HEAD_DIM)
        )
        attended, log_total = attend(query_low, key_low, value_low)
        attended_low = attended.reshape(length, local_width).astype(jnp.bfloat16)
        merge_part = jnp.dot(attended_low, merge_full, preferred_element_type=jnp.float32)
        middle_own = own_input + (branch_split(merge_part) + merge_bias_own)
        normed_two, centered_two, inverse_two = norm_split(
            middle_own, gains_own[1], shifts_own[1], full_width
        )
        hidden = (
            jnp.dot(normed_two, expand_full, preferred_element_type=jnp.float32) + expand_bias_own
        )
        sigmoid_gate = jax.nn.sigmoid(1.702 * hidden)
        activated = (hidden * sigmoid_gate).astype(jnp.bfloat16)
        shrink_part = jnp.dot(activated, shrink_full, preferred_element_type=jnp.float32)
        outputs.append(
            (middle_own + (branch_split(shrink_part) + shrink_bias_own)).astype(jnp.bfloat16)
        )
        cot_full = gather_grads(cotangent[slot_index])
        seed_full = cot_full.astype(jnp.float32) * weight_now
        seed_low = seed_full.astype(jnp.bfloat16)
        seed_own = own_slice(seed_full, col_start, local_width)
        shrink_bias_grad = shrink_bias_grad + jnp.sum(
            own_slice(seed_low, col_start, local_width).astype(jnp.float32), axis=0
        )
        shrink_grad = shrink_grad + jnp.einsum(
            "tf,td->fd", activated, seed_low, preferred_element_type=jnp.float32
        )
        act_grad = jnp.einsum(
            "td,fd->tf", seed_low, shrink_full, preferred_element_type=jnp.float32
        )
        derivative = sigmoid_gate + 1.702 * hidden * sigmoid_gate * (1.0 - sigmoid_gate)
        hidden_grad = (act_grad * derivative).astype(jnp.bfloat16)
        expand_bias_grad = expand_bias_grad + jnp.sum(hidden_grad.astype(jnp.float32), axis=0)
        expand_grad = expand_grad + jnp.einsum(
            "td,tf->df", normed_two, hidden_grad, preferred_element_type=jnp.float32
        )
        norm_part = jnp.einsum(
            "tf,df->td", hidden_grad, expand_full, preferred_element_type=jnp.float32
        )
        norm_result, gain_sum, shift_sum = norm_back_split(
            norm_part, centered_two, inverse_two, gains_own[1], full_width
        )
        middle_grad = seed_own + norm_result
        branch_grad = gather_grads(middle_grad.astype(jnp.bfloat16))
        gain_grad = gain_grad.at[1].add(gain_sum)
        shift_grad = shift_grad.at[1].add(shift_sum)
        merge_bias_grad = merge_bias_grad + jnp.sum(
            own_slice(branch_grad, col_start, local_width).astype(jnp.float32), axis=0
        )
        merge_grad = merge_grad + jnp.einsum(
            "tf,td->fd", attended_low, branch_grad, preferred_element_type=jnp.float32
        )
        attended_grad = (
            jnp.einsum("td,fd->tf", branch_grad, merge_full, preferred_element_type=jnp.float32)
            .astype(jnp.bfloat16)
            .reshape(length, local_heads, HEAD_DIM)
        )
        query_grad, key_grad, value_grad = attend_back(
            query_low, key_low, value_low, log_total, attended_grad
        )
        mixed_grad = jnp.stack(
            [
                query_grad.reshape(length, local_width).astype(jnp.float32) * HEAD_DIM ** (-0.5),
                key_grad.reshape(length, local_width).astype(jnp.float32),
                value_grad.reshape(length, local_width).astype(jnp.float32),
            ],
            axis=1,
        ).astype(jnp.bfloat16)
        heads_bias_grad = heads_bias_grad + jnp.stack(
            [
                jnp.sum(mixed_grad[:, 0].astype(jnp.float32), axis=0),
                jnp.sum(mixed_grad[:, 2].astype(jnp.float32), axis=0),
            ]
        )
        heads_grad = heads_grad + jnp.einsum(
            "td,tkf->dkf", normed, mixed_grad, preferred_element_type=jnp.float32
        )
        first_part = jnp.einsum(
            "tkf,dkf->td", mixed_grad, heads_full, preferred_element_type=jnp.float32
        )
        norm_result, gain_sum, shift_sum = norm_back_split(
            first_part, centered_one, inverse_one, gains_own[0], full_width
        )
        input_grads.append(middle_grad + norm_result)
        gain_grad = gain_grad.at[0].add(gain_sum)
        shift_grad = shift_grad.at[0].add(shift_sum)
    weight_sums = (
        lax.psum_scatter(
            heads_grad.astype(jnp.bfloat16), "row", scatter_dimension=0, tiled=True
        ).astype(jnp.float32),
        lax.psum_scatter(
            merge_grad.astype(jnp.bfloat16), "row", scatter_dimension=1, tiled=True
        ).astype(jnp.float32),
        lax.psum_scatter(
            expand_grad.astype(jnp.bfloat16), "row", scatter_dimension=0, tiled=True
        ).astype(jnp.float32),
        lax.psum_scatter(
            shrink_grad.astype(jnp.bfloat16), "row", scatter_dimension=1, tiled=True
        ).astype(jnp.float32),
    )
    weight_sums = (
        lax.psum(weight_sums[0].astype(jnp.bfloat16), "dp").astype(jnp.float32),
        lax.psum(weight_sums[1].astype(jnp.bfloat16), "dp").astype(jnp.float32),
        lax.psum(weight_sums[2].astype(jnp.bfloat16), "dp").astype(jnp.float32),
        lax.psum(weight_sums[3].astype(jnp.bfloat16), "dp").astype(jnp.float32),
    )
    small_totals = lax.psum(
        (
            heads_bias_grad,
            merge_bias_grad,
            expand_bias_grad,
            shrink_bias_grad,
            gain_grad,
            shift_grad,
        ),
        ("dp", "row"),
    )
    return (
        jnp.stack(outputs),
        jnp.stack(input_grads),
        weight_sums[0],
        small_totals[0],
        weight_sums[1],
        small_totals[1],
        weight_sums[2],
        small_totals[2],
        weight_sums[3],
        small_totals[3],
        small_totals[4],
        small_totals[5],
    )


def solution(mesh):
    placed = (
        P(("dp", "row"), None, "col"),
        P(("dp", "row"), None, "col"),
        P(("dp", "row")),
        P("row", None, "col"),
        P(None, "col"),
        P("col", "row"),
        P("col"),
        P("row", "col"),
        P("col"),
        P("col", "row"),
        P("col"),
        P(None, "col"),
        P(None, "col"),
    )
    return jax.shard_map(
        shards,
        mesh=mesh,
        in_specs=placed,
        out_specs=(
            P(("dp", "row"), None, "col"),
            P(("dp", "row"), None, "col"),
            P("row", None, "col"),
            P(None, "col"),
            P("col", "row"),
            P("col"),
            P("row", "col"),
            P("col"),
            P("col", "row"),
            P("col"),
            P(None, "col"),
            P(None, "col"),
        ),
        check_vma=False,
    )
```

profile of v0, /device:TPU:0, one launch (start us, length us, event | category | flops | bytes accessed | tf_op | source)
XLA Modules:
  0.0 845.2 jit_solution(18113840407815767616)
XLA Ops:
  8.8 4.8 fusion.140
  17.9 3.7 all-reduce.12
  26.4 9.3 %all-gather.35.cloned.1.call-done = bf16[577,1024]{1,0:T(8,128)(2,1)} async-done(((bf16[577,512]{1,0:T(8,128)(2,1)}), bf16[577,1024]{1,0:T(8,128)(2,1)}) %all-gather.35.cloned.1.call-update) | async-done | bytes 1181712 | tf_op jit(solution)/shard_map/all_gather | solution.py:36
  35.7 66.2 %all-gather.25.cloned.1.call-done = bf16[1024,3,512]{2,0,1:T(8,128)(2,1)} async-done(((bf16[256,3,512]{2,0,1:T(8,128)(2,1)}), bf16[1024,3,512]{2,0,1:T(8,128)(2,1)}) %all-gather.25.cloned.1.call-update) | async-done | bytes 3145744 | tf_op jit(solution)/shard_map/all_gather | solution.py:119
  101.9 4.3 fusion.88
  107.9 4.1 all-gather.23.cloned.1.call-done
  112.0 4.3 fusion.92
  122.0 6.5 fusion.145
  132.0 3.2 copy.85
  138.0 6.2 exponential_reduce_fusion
  145.9 4.2 fusion.34
  150.1 3.3 convolution_convert_fusion.3
  153.9 3.4 fusion.144
  166.6 3.7 fusion.139
  173.1 3.4 reduce-scatter.13.cloned.1.call-done
  179.8 3.4 all-reduce.11
  186.0 14.7 %psum.133 = s32[2]{0:T(128)S(1)} all-reduce(s32[2]{0:T(128)S(1)} %fusion.120), channel_id=1, replica_groups=mesh['dp'=4,'row'=4,'col'=2] {'dp','row'}, use_global_device_ids=true, to_apply=%region_17.18 | all-reduce | flops 2 | bytes 16 | tf_op jit(solution)/shard_map/psum | solution.py:125
  201.6 4.2 convert_multiply_fusion.1
  205.7 4.2 convert_multiply_fusion
  210.0 74.1 %all-gather.31.cloned.1.call-done = bf16[1024,2048]{1,0:T(8,128)(2,1)} async-done(((bf16[256,2048]{1,0:T(8,128)(2,1)}), bf16[1024,2048]{1,0:T(8,128)(2,1)}) %all-gather.31.cloned.1.call-update) | async-done | bytes 4194320 | tf_op jit(solution)/shard_map/all_gather | solution.py:121
  284.1 9.2 %all-gather.37.cloned.1.call-done = bf16[577,1024]{1,0:T(8,128)(2,1)} async-done(((bf16[577,512]{1,0:T(8,128)(2,1)}), bf16[577,1024]{1,0:T(8,128)(2,1)}) %all-gather.37.cloned.1.call-update) | async-done | bytes 1181712 | tf_op jit(solution)/shard_map/all_gather | solution.py:36
  293.3 7.4 fusion.147
  300.7 75.9 %all-gather.33.cloned.1.call-done = bf16[2048,1024]{1,0:T(8,128)(2,1)} async-done(((bf16[2048,256]{1,0:T(8,128)(2,1)}), bf16[2048,1024]{1,0:T(8,128)(2,1)}) %all-gather.33.cloned.1.call-update) | async-done | bytes 4194320 | tf_op jit(solution)/shard_map/all_gather | solution.py:122
  376.6 8.6 %convert_reduce_fusion = (f32[2048]{0:T(1024)}, bf16[577,2048]{1,0:T(8,128)(2,1)S(1)}) fusion(f32[577,2048]{1,0:T(8,128)} %fusion.147, f32[2048]{0:T(1024)S(1)} %convert_element_type.388, bf16[2048,1024]{1,0:T(8,128)(2,1)} %all-gather.33.cloned.1.call-done, bf16[1,577,1024]{2,1,0:T(8,128)(2,1)} %get-tuple-element.297), kind=kOutput, calls=%fused_computation.13 | convolution fusion | flops 2435473408 | bytes 12482560 | tf_op jit(solution)/shard_map/td,fd->tf/dot_general | solution.py:193
  386.7 3.7 convolution_convert_fusion
  390.8 4.9 fusion.146
  395.8 4.8 convert_reduce_fusion.1
  402.0 3.7 convolution_convert_fusion.1
  405.8 7.4 convolution_convert_fusion.4
  413.3 7.3 convolution_convert_fusion.2
  420.7 2.9 fusion.78
  423.6 3.7 all-reduce.10
  427.4 3.8 fusion.133
  431.3 5.6 reduce-scatter.19.cloned.1.call-done
  436.9 3.6 fusion.135
  440.6 8.7 %all-gather.39.cloned.1.call-done = bf16[577,1024]{1,0:T(8,128)(2,1)} async-done(((bf16[577,512]{1,0:T(8,128)(2,1)}), bf16[577,1024]{1,0:T(8,128)(2,1)}) %all-gather.39.cloned.1.call-update) | async-done | bytes 1181712 | tf_op jit(solution)/shard_map/all_gather | solution.py:54
  449.4 3.8 fusion.148
  453.1 8.1 all-gather.41.cloned.1.call-done
  461.2 3.9 add_convert_fusion.3
  465.3 5.6 fusion.84
  470.9 8.0 add_convert_fusion
  479.2 5.7 fusion.149
  484.9 5.2 add_convert_fusion.1
  491.5 2.9 convolution_convert_fusion.10
  498.4 7.3 fusion.31
  506.9 7.3 fusion.37
  516.3 6.0 multiply_reduce_fusion
  522.4 6.1 multiply_convert_fusion
  532.1 4.8 fusion.42
  539.2 5.9 multiply_reduce_fusion.1
  545.1 6.2 multiply_convert_fusion.1
  555.0 3.9 fusion.45
  560.0 4.4 fusion.90
  564.5 4.6 add_convert_fusion.2
  569.2 5.4 bitcast_convert_fusion
  574.6 5.3 bitcast_convert_fusion.1
  585.3 65.7 %reduce-scatter.33.cloned.1.call-done = bf16[256,2048]{1,0:T(8,128)(2,1)} async-done(((bf16[1024,2048]{1,0:T(8,128)(2,1)}), bf16[256,2048]{1,0:T(8,128)(2,1)}) %reduce-scatter.33.cloned.1.call-update) | async-done | bytes 1048592 | tf_op jit(solution)/shard_map/reduce_scatter | solution.py:259
  651.0 63.2 %reduce-scatter.29.cloned.1.call-done = bf16[256,3,512]{2,0,1:T(8,128)(2,1)} async-done(((bf16[1024,3,512]{2,0,1:T(8,128)(2,1)}), bf16[256,3,512]{2,0,1:T(8,128)(2,1)}) %reduce-scatter.29.cloned.1.call-update) | async-done | bytes 786448 | tf_op jit(solution)/shard_map/reduce_scatter | solution.py:253
  716.8 9.0 %reduce-scatter.27.cloned.1.call-done = bf16[577,512]{1,0:T(8,128)(2,1)} async-done(((bf16[577,1024]{1,0:T(8,128)(2,1)}), bf16[577,512]{1,0:T(8,128)(2,1)}) %reduce-scatter.27.cloned.1.call-update) | async-done | bytes 590864 | tf_op jit(solution)/shard_map/reduce_scatter | solution.py:40
  725.8 12.6 %reduce-scatter.23.cloned.1.call-done = bf16[577,512]{1,0:T(8,128)(2,1)} async-done(((bf16[577,1024]{1,0:T(8,128)(2,1)}), bf16[577,512]{1,0:T(8,128)(2,1)}) %reduce-scatter.23.cloned.1.call-update) | async-done | bytes 590864 | tf_op jit(solution)/shard_map/reduce_scatter | solution.py:40
  741.2 3.3 all-reduce.9
  747.1 3.2 copy.110
  750.3 78.3 %all-reduce.8 = (f32[2,512]{1,0:T(2,128)}, f32[512]{0:T(512)}, f32[2048]{0:T(1024)}, f32[512]{0:T(512)}, f32[2,512]{1,0:T(2,128)}, /*index=5*/f32[2,512]{1,0:T(2,128)}) all-reduce(f32[2,512]{1,0:T(2,128)S(1)} %maximum_add_fusion, f32[512]{0:T(512)S(1)} %add.530, ...), channel_id=1, replica_groups=mesh['dp'=4,'row'=4,'col'=2] {'dp','row'}, use_global_device_ids=true, to_apply=%region_47.48 | all-reduce | flops 6144 | bytes 49152 | tf_op jit(solution)/shard_map/psum | solution.py:272
  828.6 3.3 all-reduce.16.cloned.1.call-done
  (319 shorter events, 86.9 us)
Async XLA Ops:
  7.2 28.5 %all-gather.35.cloned.1.call-start = ((), (), s32[]{:S(2)}) async-start(), calls=%async_computation.20 | async-start | bytes 1794048 | tf_op jit(solution)/shard_map/all_gather | solution.py:36
  8.0 13.8 %copy-start.55 = (f32[1,512]{1,0:T(1,128)}, f32[1,512]{1,0:T(1,128)S(1)}, u32[]{:S(2)}) copy-start(f32[1,512]{1,0:T(1,128)S(1)} %get-tuple-element.329) | copy-start | bytes 6148
  8.8 4.8 copy-start.70
  23.9 78.1 %all-gather.25.cloned.1.call-start = ((), (), s32[]{:S(2)}) async-start(), calls=%async_computation.13 | async-start | bytes 3932160 | tf_op jit(solution)/shard_map/all_gather | solution.py:119
  24.6 87.4 %all-gather.23.cloned.1.call-start = ((), (), s32[]{:S(2)}) async-start(), calls=%async_computation.12 | async-start | bytes 1794048 | tf_op jit(solution)/shard_map/all_gather | solution.py:36
  25.3 124.7 %all-gather.27.cloned.1.call-start = ((), (), s32[]{:S(2)}) async-start(), calls=%async_computation.14 | async-start | bytes 1310720 | tf_op jit(solution)/shard_map/all_gather | solution.py:120
  25.9 147.2 %reduce-scatter.17.cloned.1.call-start = ((), (), s32[]{:S(2)}) async-start(), calls=%async_computation.21 | async-start | bytes 1794048 | tf_op jit(solution)/shard_map/reduce_scatter | solution.py:58
  26.4 127.5 %copy-start.45 = (f32[8,64]{1,0:T(8,128)}, f32[8,64]{1,0:T(8,128)S(1)}, u32[]{:S(2)}) copy-start(f32[8,64]{1,0:T(8,128)S(1)} %add.478) | copy-start | bytes 6148
  120.0 8.4 copy-start.14
  121.9 6.5 copy-start.10
  130.1 23.8 %copy-start.12 = (bf16[577,1,512]{0,2,1:T(8,128)(2,1)}, bf16[577,1,512]{0,2,1:T(8,128)(2,1)S(1)}, u32[]{:S(2)}) copy-start(bf16[577,1,512]{0,2,1:T(8,128)(2,1)S(1)} %copy.86) | copy-start | bytes 1772548
  132.0 27.0 %copy-start.6 = (f32[577,1,512]{0,2,1:T(8,128)}, f32[577,1,512]{0,2,1:T(8,128)S(1)}, u32[]{:S(2)}) copy-start(f32[577,1,512]{0,2,1:T(8,128)S(1)} %copy.84) | copy-start | bytes 3545092
  138.0 7.9 copy-start
  153.4 23.1 %reduce-scatter.13.cloned.1.call-start = ((), (), s32[]{:S(2)}) async-start(), calls=%async_computation.15 | async-start | bytes 1794048 | tf_op jit(solution)/shard_map/reduce_scatter | solution.py:58
  166.5 35.0 %all-gather.43.cloned.1.call-start = ((), (), s32[]{:S(2)}) async-start(), calls=%async_computation.34 | async-start | bytes 1794048 | tf_op jit(solution)/shard_map/all_gather | solution.py:54
  171.2 34.5 %all-gather.45.cloned.1.call-start = ((), (), s32[]{:S(2)}) async-start(), calls=%async_computation.35 | async-start | bytes 1794048 | tf_op jit(solution)/shard_map/all_gather | solution.py:54
  172.3 111.8 %all-gather.31.cloned.1.call-start = ((), (), s32[]{:S(2)}) async-start(), calls=%async_computation.17 | async-start | bytes 5242880 | tf_op jit(solution)/shard_map/all_gather | solution.py:121
  173.0 120.3 %all-gather.37.cloned.1.call-start = ((), (), s32[]{:S(2)}) async-start(), calls=%async_computation.22 | async-start | bytes 1794048 | tf_op jit(solution)/shard_map/all_gather | solution.py:36
  173.1 5.4 copy-start.4
  185.1 15.6 %copy-start.59 = (bf16[2048]{0:T(1024)(128)(2,1)S(1)}, bf16[2048]{0:T(1024)(128)(2,1)}, u32[]{:S(2)}) copy-start(bf16[2048]{0:T(1024)(128)(2,1)} %param.37) | copy-start | bytes 12292
  185.2 191.4 %all-gather.33.cloned.1.call-start = ((), (), s32[]{:S(2)}) async-start(), calls=%async_computation.18 | async-start | bytes 5242880 | tf_op jit(solution)/shard_map/all_gather | solution.py:122
  185.9 204.9 %all-gather.29.cloned.1.call-start = ((), (), s32[]{:S(2)}) async-start(), calls=%async_computation.16 | async-start | bytes 1794048 | tf_op jit(solution)/shard_map/all_gather | solution.py:36
  210.0 210.8 %reduce-scatter.25.cloned.1.call-start = ((), (), s32[]{:S(2)}) async-start(), calls=%async_computation.27 | async-start | bytes 1794048 | tf_op jit(solution)/shard_map/reduce_scatter | solution.py:40
  376.6 10.1 %copy-start.63 = (bf16[1024,2048]{1,0:T(8,128)(2,1)S(1)}, bf16[1024,2048]{1,0:T(8,128)(2,1)}, u32[]{:S(2)}) copy-start(bf16[1024,2048]{1,0:T(8,128)(2,1)} %all-gather.31.cloned.1.call-done) | copy-start | bytes 12582916
  390.5 30.2 %reduce-scatter.21.cloned.1.call-start = ((), (), s32[]{:S(2)}) async-start(), calls=%async_computation.24 | async-start | bytes 1794048 | tf_op jit(solution)/shard_map/reduce_scatter | solution.py:40
  390.8 5.0 copy-start.23
  390.8 5.0 copy-start.65
  395.7 4.9 copy-start.71
  395.8 6.3 copy-start.64
  405.8 21.6 %reduce-scatter.15.cloned.1.call-start = ((), (), s32[]{:S(2)}) async-start(), calls=%async_computation.19 | async-start | bytes 1794048 | tf_op jit(solution)/shard_map/reduce_scatter | solution.py:58
  413.2 7.5 copy-start.62
  413.2 23.7 %reduce-scatter.19.cloned.1.call-start = ((), (), s32[]{:S(2)}) async-start(), calls=%async_computation.23 | async-start | bytes 1794048 | tf_op jit(solution)/shard_map/reduce_scatter | solution.py:58
  420.6 28.7 %all-gather.39.cloned.1.call-start = ((), (), s32[]{:S(2)}) async-start(), calls=%async_computation.25 | async-start | bytes 1794048 | tf_op jit(solution)/shard_map/all_gather | solution.py:54
  427.4 9.5 %copy-start.32 = (bf16[577,512]{1,0:T(8,128)(2,1)S(1)}, bf16[577,512]{1,0:T(8,128)(2,1)}, u32[]{:S(2)}) copy-start(bf16[577,512]{1,0:T(8,128)(2,1)} %reduce-scatter.25.cloned.1.call-done) | copy-start | bytes 1772548
  431.2 30.0 %all-gather.41.cloned.1.call-start = ((), (), s32[]{:S(2)}) async-start(), calls=%async_computation.28 | async-start | bytes 1794048 | tf_op jit(solution)/shard_map/all_gather | solution.py:54
  440.6 20.7 %copy-start.28 = (bf16[8,64,577]{2,1,0:T(8,128)(2,1)S(1)}, bf16[8,64,577]{2,1,0:T(8,128)(2,1)}, u32[]{:S(2)}) copy-start(bf16[8,64,577]{2,1,0:T(8,128)(2,1)} %fusion.34) | copy-start | bytes 1772548
  440.6 144.7 %reduce-scatter.31.cloned.1.call-start = ((), (), s32[]{:S(2)}) async-start(), calls=%async_computation.31 | async-start | bytes 1310720 | tf_op jit(solution)/shard_map/reduce_scatter | solution.py:256
  453.1 12.1 %copy-start.24 = (bf16[1,577,1024]{2,1,0:T(8,128)(2,1)S(1)}, bf16[1,577,1024]{2,1,0:T(8,128)(2,1)}, u32[]{:S(2)}) copy-start(bf16[1,577,1024]{2,1,0:T(8,128)(2,1)} %get-tuple-element.295) | copy-start | bytes 3545092
  465.2 120.1 %reduce-scatter.35.cloned.1.call-start = ((), (), s32[]{:S(2)}) async-start(), calls=%async_computation.33 | async-start | bytes 5242880 | tf_op jit(solution)/shard_map/reduce_scatter | solution.py:262
  465.2 5.6 copy-start.25
  478.9 6.0 copy-start.67
  479.0 172.0 %reduce-scatter.33.cloned.1.call-start = ((), (), s32[]{:S(2)}) async-start(), calls=%async_computation.32 | async-start | bytes 5242880 | tf_op jit(solution)/shard_map/reduce_scatter | solution.py:259
  479.2 5.8 copy-start.74
  490.2 223.9 %reduce-scatter.29.cloned.1.call-start = ((), (), s32[]{:S(2)}) async-start(), calls=%async_computation.30 | async-start | bytes 3932160 | tf_op jit(solution)/shard_map/reduce_scatter | solution.py:253
  498.4 7.3 copy-start.17
  498.4 8.4 copy-start.43
  506.9 9.5 %copy-start.8 = (f32[577,1,512]{0,2,1:T(8,128)S(1)}, f32[577,1,512]{0,2,1:T(8,128)}, u32[]{:S(2)}) copy-start(f32[577,1,512]{0,2,1:T(8,128)} %copy.89) | copy-start | bytes 3545092
  522.4 6.1 copy-start.11
  522.4 6.1 copy-start.46
  532.1 7.1 copy-start.7
  545.1 6.2 copy-start.9
  555.0 5.0 copy-start.38
  560.0 4.5 copy-start.41
  560.0 4.5 copy-start.66
  569.1 156.7 %reduce-scatter.27.cloned.1.call-start = ((), (), s32[]{:S(2)}) async-start(), calls=%async_computation.29 | async-start | bytes 1794048 | tf_op jit(solution)/shard_map/reduce_scatter | solution.py:40
  574.6 163.8 %reduce-scatter.23.cloned.1.call-start = ((), (), s32[]{:S(2)}) async-start(), calls=%async_computation.26 | async-start | bytes 1794048 | tf_op jit(solution)/shard_map/reduce_scatter | solution.py:40
  580.0 251.9 %all-reduce.16.cloned.1.call-start = ((), (), s32[]{:S(2)}) async-start(), calls=%async_computation.36 | async-start | bytes 6291456 | tf_op jit(solution)/shard_map/psum | solution.py:267
  715.2 23.2 %copy-start.48 = (f32[577]{0:T(1024)S(1)}, f32[577]{0:T(1024)}, u32[]{:S(2)}) copy-start(f32[577]{0:T(1024)} %copy-done.47) | copy-start | bytes 6928
  715.2 23.2 %copy-start.50 = (f32[577]{0:T(1024)S(1)}, f32[577]{0:T(1024)}, u32[]{:S(2)}) copy-start(f32[577]{0:T(1024)} %copy-done.49) | copy-start | bytes 6928
  715.2 23.2 %copy-start.52 = (f32[577]{0:T(1024)S(1)}, f32[577]{0:T(1024)}, u32[]{:S(2)}) copy-start(f32[577]{0:T(1024)} %copy-done.51) | copy-start | bytes 6928
  715.2 23.2 %copy-start.54 = (f32[577]{0:T(1024)S(1)}, f32[577]{0:T(1024)}, u32[]{:S(2)}) copy-start(f32[577]{0:T(1024)} %copy-done.53) | copy-start | bytes 6928
  715.3 23.2 %copy-start.56 = (f32[1,512]{1,0:T(1,128)S(1)}, f32[1,512]{1,0:T(1,128)}, u32[]{:S(2)}) copy-start(f32[1,512]{1,0:T(1,128)} %copy-done.55) | copy-start | bytes 6148
  716.7 27.9 %copy-start.22 = (f32[577,512]{1,0:T(8,128)S(1)}, f32[577,512]{1,0:T(8,128)}, u32[]{:S(2)}) copy-start(f32[577,512]{1,0:T(8,128)} %get-tuple-element.281) | copy-start | bytes 3545092
  725.8 18.8 %copy-start.33 = (bf16[577,512]{1,0:T(8,128)(2,1)S(1)}, bf16[577,512]{1,0:T(8,128)(2,1)}, u32[]{:S(2)}) copy-start(bf16[577,512]{1,0:T(8,128)(2,1)} %reduce-scatter.27.cloned.1.call-done) | copy-start | bytes 1772548
  (36 other events, 71.9 us)
Sparse Core Ops, SparseCore 0:
  24.0 11.6 all-gather.34
  37.3 64.6 all-gather.24
  104.0 7.9 all-gather.22
  113.4 31.3 all-gather.26
  153.5 9.7 reduce-scatter.16
  166.7 9.8 reduce-scatter.12
  178.1 10.4 all-gather.42
  190.1 10.4 all-gather.44
  202.1 81.9 all-gather.30
  285.5 7.7 all-gather.36
  294.8 81.7 all-gather.32
  378.6 7.4 all-gather.28
  390.6 7.4 reduce-scatter.24
  405.9 6.8 reduce-scatter.20
  414.9 9.8 reduce-scatter.14
  427.0 9.8 reduce-scatter.18
  438.9 10.4 all-gather.38
  450.8 10.4 all-gather.40
  465.3 28.3 reduce-scatter.30
  495.9 75.4 reduce-scatter.34
  573.7 77.2 reduce-scatter.32
  653.4 60.7 reduce-scatter.28
  717.1 8.6 reduce-scatter.26
  728.5 9.8 reduce-scatter.22
  742.1 89.7 all-reduce.15
where the time goes:
time: 851 us; the launch traced here: 845 us
  waiting for transfers between devices  422 us (50%)
  matrix products  174 us (20%)
  blocking collectives  107 us (13%)
  other arithmetic  63.1 us (7%)
  local copies, waits for them, and re-layouts  60.1 us (7%)
  between operations  16.3 us (2%)
    psum x1, blocking collectives, shards(): lax.psum((heads_bias_grad, merge_bias_grad, expand_bias_grad, shrink_bias...  78.3 us
    all_gather x1, waiting for transfers between devices, shards(): lax.all_gather(shrink_weight, 'row', axis=1, tiled=True)  75.9 us
    all_gather x1, waiting for transfers between devices, shards(): lax.all_gather(expand_weight, 'row', axis=0, tiled=True)  74.1 us
    all_gather x1, waiting for transfers between devices, shards(): lax.all_gather(heads_weight, 'row', axis=0, tiled=True)  66.2 us
    reduce_scatter x1, waiting for transfers between devices, shards(): lax.psum_scatter(expand_grad.astype(jnp.bfloat16), 'row', scatter_dimensi...  65.7 us
    reduce_scatter x1, waiting for transfers between devices, shards(): lax.psum_scatter(heads_grad.astype(jnp.bfloat16), 'row', scatter_dimensio...  63.2 us
    unnamed x167, local copies, waits for them, and re-layouts  23.8 us
    all_gather x4, waiting for transfers between devices, norm_split(): lax.all_gather(normed, 'col', axis=1, tiled=True)  22.7 us
  transfers between devices with their start and end apart: 25, of which 15 were waited for; matrix products, arithmetic and copies ran while one was open for 30% of the time, Pallas kernels for 0%

commit v1 on v0

v1 whole, which is shorter than its diff:
```python
import functools

import jax
import jax.numpy as jnp
from jax import lax
from jax.experimental import pallas as pl
from jax.experimental.pallas import tpu as pltpu
from jax.sharding import PartitionSpec as P

HEAD_DIM = 64
MICRO = 2
BF16 = jnp.bfloat16
F32 = jnp.float32
VMEM_LIMIT = 56 << 20


def peer(value, axis, p):
    n = lax.axis_size(axis)
    return lax.ppermute(value, axis, [(i, i ^ p) for i in range(n)])


def xor_order(value, dim, axis):
    n = lax.axis_size(axis)
    index = lax.axis_index(axis)
    size = value.shape[dim]
    bit = 1
    while bit < n:
        run = size * bit // n
        pieces = [lax.slice_in_dim(value, at, at + run, axis=dim) for at in range(0, size, run)]
        swapped = lax.concatenate([pieces[k ^ 1] for k in range(len(pieces))], dim)
        value = jnp.where((index & bit) != 0, swapped, value)
        bit *= 2
    return value


def cut(value, dim, n, k):
    run = value.shape[dim] // n
    return lax.slice_in_dim(value, k * run, (k + 1) * run, axis=dim)


def col_full(own, feature_dim):
    n_col = lax.axis_size("col")
    if n_col != 2:
        return xor_order(lax.all_gather(own, "col", axis=feature_dim, tiled=True), feature_dim, "row")
    other = peer(own, "col", 1)
    first = lax.axis_index("col") == 0
    full = lax.concatenate(
        [jnp.where(first, own, other), jnp.where(first, other, own)], feature_dim
    )
    return xor_order(full, feature_dim, "row")


def col_own(full, feature_dim):
    n_col = lax.axis_size("col")
    width = full.shape[feature_dim] // n_col
    plain = xor_order(full, feature_dim, "row")
    if n_col == 2:
        low = lax.slice_in_dim(plain, 0, width, axis=feature_dim)
        high = lax.slice_in_dim(plain, width, 2 * width, axis=feature_dim)
        return jnp.where(lax.axis_index("col") == 0, low, high)
    return lax.dynamic_slice_in_dim(plain, lax.axis_index("col") * width, width, feature_dim)


def col_sum(part):
    low = part.astype(BF16)
    if lax.axis_size("col") == 2:
        return low.astype(F32) + peer(low, "col", 1).astype(F32)
    return lax.psum(low, "col").astype(F32)


def col_sum_own(part):
    low = part.astype(BF16)
    if lax.axis_size("col") == 2:
        plain = xor_order(low, low.ndim - 1, "row")
        width = plain.shape[-1] // 2
        first = lax.axis_index("col") == 0
        head, tail = plain[..., :width], plain[..., width:]
        kept = jnp.where(first, head, tail)
        other = peer(jnp.where(first, tail, head), "col", 1)
        return kept.astype(F32) + other.astype(F32)
    return col_own(lax.psum(low, "col").astype(F32), low.ndim - 1)


def gather_weight(own, inner_dim, model_dim):
    n_dp, n_row = lax.axis_size("dp"), lax.axis_size("row")
    own = xor_order(own, inner_dim, "dp")
    quarter = cut(own, inner_dim, n_dp, 0)
    over_row = lax.concatenate([peer(quarter, "row", j) for j in range(1, n_row)], model_dim)
    rest = [over_row] + [peer(over_row, "dp", p) for p in range(1, n_dp)]
    return lax.concatenate([own, lax.concatenate(rest, inner_dim)], model_dim)


def reduce_weight(grad, inner_dim, model_dim):
    n_dp, n_row = lax.axis_size("dp"), lax.axis_size("row")
    total = cut(grad, inner_dim, n_dp, 0).astype(F32)
    for p in range(1, n_dp):
        total = total + peer(cut(grad, inner_dim, n_dp, p), "dp", p).astype(F32)
    part = total.astype(BF16)
    total = cut(part, model_dim, n_row, 0).astype(F32)
    for j in range(1, n_row):
        total = total + peer(cut(part, model_dim, n_row, j), "row", j).astype(F32)
    part = total.astype(BF16)
    whole = lax.concatenate([part] + [peer(part, "dp", p) for p in range(1, n_dp)], inner_dim)
    return xor_order(whole, inner_dim, "dp").astype(F32)


def sum_all(value):
    for axis in ("dp", "row"):
        bit = 1
        while bit < lax.axis_size(axis):
            value = value + peer(value, axis, bit)
            bit *= 2
    return value


def head_mask(rows, width, h, count):
    lane = lax.broadcasted_iota(jnp.int32, (rows, width), 1)
    return (lane >= h * HEAD_DIM) & (lane < (h + 1) * HEAD_DIM)


def nt(a, b):
    return lax.dot_general(a, b, (((1,), (1,)), ((), ())), preferred_element_type=F32)


def nn(a, b):
    return lax.dot_general(a, b, (((1,), (0,)), ((), ())), preferred_element_type=F32)


def attend_kernel(length, q_ref, k_ref, v_ref, o_ref):
    rows, width = q_ref.shape
    count = width // HEAD_DIM
    k = k_ref[...]
    v = v_ref[...]
    chunk = 256
    for start in range(0, rows, chunk):
        size = min(chunk, rows - start)
        q = q_ref[pl.ds(start, size), :]
        result = None
        for h in range(count):
            mask = head_mask(size, width, h, count)
            scores = nt(jnp.where(mask, q, jnp.zeros_like(q)), k)
            key = lax.broadcasted_iota(jnp.int32, scores.shape, 1)
            scores = jnp.where(key < length, scores, -1e30)
            top = jnp.max(scores, axis=1, keepdims=True)
            grown = jnp.exp(scores - top)
            total = jnp.sum(grown, axis=1, keepdims=True)
            out = nn(grown.astype(BF16), v) / total
            result = out if result is None else jnp.where(mask, out, result)
        o_ref[pl.ds(start, size), :] = result.astype(BF16)


def attend(q, k, v, length):
    count, rows, width = q.shape
    block = min(width, 2 * HEAD_DIM)
    spec = pl.BlockSpec((None, rows, block), lambda i, b: (i, 0, b))
    flops = 4 * count * rows * rows * width
    return pl.pallas_call(
        functools.partial(attend_kernel, length),
        grid=(count, width // block),
        in_specs=[spec] * 3,
        out_specs=spec,
        out_shape=jax.ShapeDtypeStruct(q.shape, BF16),
        compiler_params=pltpu.CompilerParams(vmem_limit_bytes=VMEM_LIMIT),
        cost_estimate=pl.CostEstimate(
            flops=flops, bytes_accessed=8 * q.size, transcendentals=count * rows * rows * width // 64
        ),
        name="attend",
    )(q, k, v)


def attend_back_kernel(length, q_ref, k_ref, v_ref, up_ref, dq_ref, dk_ref, dv_ref, probs, grads, q_all, up_all):
    rows, width = q_ref.shape
    count = width // HEAD_DIM
    lanes = probs.shape[1] // count
    k = k_ref[...]
    v = v_ref[...]
    chunk = 256
    for h in range(count):
        base = h * lanes
        if rows < lanes:
            probs[:, pl.ds(base + rows, lanes - rows)] = jnp.zeros((rows, lanes - rows), BF16)
            grads[:, pl.ds(base + rows, lanes - rows)] = jnp.zeros((rows, lanes - rows), BF16)
            q_all[pl.ds(base + rows, lanes - rows), :] = jnp.zeros((lanes - rows, width), BF16)
            up_all[pl.ds(base + rows, lanes - rows), :] = jnp.zeros((lanes - rows, width), BF16)
        for start in range(0, rows, chunk):
            size = min(chunk, rows - start)
            mask = head_mask(size, width, h, count)
            q = q_ref[pl.ds(start, size), :]
            up = up_ref[pl.ds(start, size), :]
            q = jnp.where(mask, q, jnp.zeros_like(q))
            up = jnp.where(mask, up, jnp.zeros_like(up))
            q_all[pl.ds(base + start, size), :] = q
            up_all[pl.ds(base + start, size), :] = up
            scores = nt(k, q)
            key = lax.broadcasted_iota(jnp.int32, scores.shape, 0)
            scores = jnp.where(key < length, scores, -1e30)
            top = jnp.max(scores, axis=0, keepdims=True)
            grown = jnp.exp(scores - top)
            share = grown * (1.0 / jnp.sum(grown, axis=0, keepdims=True))
            prob_grad = nt(v, up)
            delta = jnp.sum(share * prob_grad, axis=0, keepdims=True)
            probs[:, pl.ds(base + start, size)] = share.astype(BF16)
            grads[:, pl.ds(base + start, size)] = (share * (prob_grad - delta)).astype(BF16)
    dv_ref[...] = nn(probs[...], up_all[...]).astype(BF16)
    dk_ref[...] = nn(grads[...], q_all[...]).astype(BF16)
    turned = k.astype(F32).T.astype(BF16)
    pieces = []
    for h in range(count):
        pieces.append(nn(turned[h * HEAD_DIM : (h + 1) * HEAD_DIM, :], grads[:, pl.ds(h * lanes, rows)]))
    dq = jnp.concatenate(pieces, axis=0).T if count > 1 else pieces[0].T
    dq_ref[...] = (dq.astype(BF16).astype(F32) * HEAD_DIM**-0.5).astype(BF16)


def attend_back(q, k, v, up, length):
    count, rows, width = q.shape
    block = min(width, 2 * HEAD_DIM)
    lanes = -(-rows // 128) * 128
    heads = block // HEAD_DIM
    spec = pl.BlockSpec((None, rows, block), lambda i, b: (i, 0, b))
    shape = jax.ShapeDtypeStruct(q.shape, BF16)
    return pl.pallas_call(
        functools.partial(attend_back_kernel, length),
        grid=(count, width // block),
        in_specs=[spec] * 4,
        out_specs=[spec] * 3,
        out_shape=[shape] * 3,
        scratch_shapes=[
            pltpu.VMEM((rows, heads * lanes), BF16),
            pltpu.VMEM((rows, heads * lanes), BF16),
            pltpu.VMEM((heads * lanes, block), BF16),
            pltpu.VMEM((heads * lanes, block), BF16),
        ],
        compiler_params=pltpu.CompilerParams(vmem_limit_bytes=VMEM_LIMIT),
        cost_estimate=pl.CostEstimate(
            flops=10 * count * rows * rows * width,
            bytes_accessed=14 * q.size,
            transcendentals=count * rows * rows * width // 64,
        ),
        name="attend_back",
    )(q, k, v, up)


def norm_forward(values, gain, shift):
    mean = jnp.mean(values, axis=-1, keepdims=True)
    centered = values - mean
    inverse = lax.rsqrt(jnp.mean(centered * centered, axis=-1, keepdims=True) + 1e-05)
    xhat = centered * inverse
    return (xhat * gain + shift).astype(BF16), mean, inverse


def norm_back(upstream, values, mean, inverse, gain):
    xhat = (values - mean) * inverse
    scaled = upstream * gain
    first = jnp.mean(scaled, axis=-1, keepdims=True)
    second = jnp.mean(scaled * xhat, axis=-1, keepdims=True)
    grad = inverse * (scaled - first - xhat * second)
    return grad, jnp.sum(upstream * xhat, axis=(0, 1)), jnp.sum(upstream, axis=(0, 1))


def shards(
    images,
    cotangent,
    micro_batch,
    heads_weight,
    heads_bias,
    merge_weight,
    merge_bias,
    expand_weight,
    expand_bias,
    shrink_weight,
    shrink_bias,
    norm_gains,
    norm_shifts,
):
    count, length, width = images.shape
    rows = -(-length // 16) * 16
    pad = ((0, 0), (0, rows - length), (0, 0))

    heads_full = gather_weight(jnp.transpose(heads_weight, (1, 0, 2)), 2, 1)
    x_own = jnp.pad(images, pad)
    x_low = col_full(x_own, 2)
    params = jnp.concatenate(
        [norm_gains, norm_shifts, merge_bias[None], shrink_bias[None]], axis=0
    )
    params = col_full(params, 1).astype(F32)
    gain_one, gain_two, shift_one, shift_two, merge_bias_full, shrink_bias_full = (
        params[k] for k in range(6)
    )
    merge_full = gather_weight(merge_weight, 0, 1)
    cot_low = col_full(jnp.pad(cotangent, pad), 2)
    expand_full = gather_weight(expand_weight, 1, 0)
    shrink_full = gather_weight(shrink_weight, 0, 1)
    heads_bias_own = xor_order(heads_bias, 1, "dp").astype(F32)
    expand_bias_own = xor_order(expand_bias, 0, "dp").astype(F32)

    member = (micro_batch[:, None] == jnp.arange(MICRO, dtype=jnp.int32)[None, :]).astype(jnp.int32)
    totals = lax.psum(jnp.sum(member, axis=0), ("dp", "row"))
    all_slots = count * lax.axis_size("dp") * lax.axis_size("row")
    batch_weight = all_slots / (MICRO * totals.astype(F32))
    slot_weight = jnp.sum(member.astype(F32) * batch_weight[None, :], axis=1)

    x = x_low.astype(F32)
    normed, mean_one, inverse_one = norm_forward(x, gain_one, shift_one)
    mixed = jnp.einsum("itd,kdf->kitf", normed, heads_full, preferred_element_type=F32)
    query = ((mixed[0] + heads_bias_own[0]) * HEAD_DIM**-0.5).astype(BF16)
    key = mixed[1].astype(BF16)
    value = (mixed[2] + heads_bias_own[1]).astype(BF16)
    attended = attend(query, key, value, length)
    merge_part = jnp.einsum("itf,fd->itd", attended, merge_full, preferred_element_type=F32)
    middle = x + (col_sum(merge_part) + merge_bias_full)
    normed_two, mean_two, inverse_two = norm_forward(middle, gain_two, shift_two)
    hidden = (
        jnp.einsum("itd,dh->ith", normed_two, expand_full, preferred_element_type=F32)
        + expand_bias_own
    )
    gate = jax.nn.sigmoid(1.702 * hidden)
    activated = (hidden * gate).astype(BF16)
    slope = (gate + 1.702 * hidden * gate * (1.0 - gate)).astype(BF16)
    seed = cot_low.astype(F32) * slot_weight[:, None, None]
    seed_low = seed.astype(BF16)

    shrink_grad = jnp.einsum("ith,itd->hd", activated, seed_low, preferred_element_type=F32)
    shrink_sum = reduce_weight(shrink_grad.astype(BF16), 0, 1)
    act_grad = jnp.einsum("itd,hd->ith", seed_low, shrink_full, preferred_element_type=F32)
    hidden_grad = (act_grad * slope.astype(F32)).astype(BF16)
    norm_part = jnp.einsum("ith,dh->itd", hidden_grad, expand_full, preferred_element_type=F32)
    normed_two_grad = col_sum(norm_part)
    expand_grad = jnp.einsum("itd,ith->dh", normed_two, hidden_grad, preferred_element_type=F32)
    expand_sum = reduce_weight(expand_grad.astype(BF16), 1, 0)
    result, gain_sum_two, shift_sum_two = norm_back(
        normed_two_grad, middle, mean_two, inverse_two, gain_two
    )
    middle_grad = seed + result
    branch_grad = middle_grad.astype(BF16)

    shrink_part = jnp.einsum("ith,hd->itd", activated, shrink_full, preferred_element_type=F32)
    output = (
        col_own(middle, 2) + (col_sum_own(shrink_part) + shrink_bias.astype(F32))
    ).astype(BF16)[:, :length]

    attended_grad = jnp.einsum(
        "itd,fd->itf", branch_grad, merge_full, preferred_element_type=F32
    ).astype(BF16)
    merge_grad = jnp.einsum("itf,itd->fd", attended, branch_grad, preferred_element_type=F32)
    merge_sum = reduce_weight(merge_grad.astype(BF16), 0, 1)
    grads = attend_back(query, key, value, attended_grad, length)
    mixed_grad = jnp.stack(grads)
    heads_grad = jnp.einsum("itd,kitf->kdf", normed, mixed_grad, preferred_element_type=F32)
    heads_sum = reduce_weight(heads_grad.astype(BF16), 2, 1)
    first_part = jnp.einsum("kitf,kdf->itd", mixed_grad, heads_full, preferred_element_type=F32)
    normed_grad = col_sum(first_part)
    result, gain_sum_one, shift_sum_one = norm_back(normed_grad, x, mean_one, inverse_one, gain_one)
    input_grad = col_own(middle_grad + result, 2)[:, :length]

    model_sums = jnp.stack(
        [
            gain_sum_one,
            gain_sum_two,
            shift_sum_one,
            shift_sum_two,
            jnp.sum(branch_grad.astype(F32), axis=(0, 1)),
            jnp.sum(seed_low.astype(F32), axis=(0, 1)),
        ]
    )
    model_sums = col_own(model_sums, 1)
    heads_bias_grad = xor_order(
        jnp.stack(
            [jnp.sum(grads[0].astype(F32), axis=(0, 1)), jnp.sum(grads[2].astype(F32), axis=(0, 1))]
        ),
        1,
        "dp",
    )
    expand_bias_grad = xor_order(jnp.sum(hidden_grad.astype(F32), axis=(0, 1)), 0, "dp")
    packed = sum_all(
        jnp.concatenate([model_sums.ravel(), heads_bias_grad.ravel(), expand_bias_grad])
    )
    model_sums = packed[: 6 * width].reshape(6, width)
    heads_bias_grad = packed[6 * width : 8 * width].reshape(2, width)
    expand_bias_grad = packed[8 * width :]
    return (
        output,
        input_grad,
        jnp.transpose(heads_sum, (1, 0, 2)),
        heads_bias_grad,
        merge_sum,
        model_sums[4],
        expand_sum,
        expand_bias_grad,
        shrink_sum,
        model_sums[5],
        model_sums[0:2],
        model_sums[2:4],
    )


def solution(mesh):
    placed = (
        P(("dp", "row"), None, "col"),
        P(("dp", "row"), None, "col"),
        P(("dp", "row")),
        P("row", None, "col"),
        P(None, "col"),
        P("col", "row"),
        P("col"),
        P("row", "col"),
        P("col"),
        P("col", "row"),
        P("col"),
        P(None, "col"),
        P(None, "col"),
    )
    return jax.shard_map(
        shards,
        mesh=mesh,
        in_specs=placed,
        out_specs=(
            P(("dp", "row"), None, "col"),
            P(("dp", "row"), None, "col"),
            P("row", None, "col"),
            P(None, "col"),
            P("col", "row"),
            P("col"),
            P("row", "col"),
            P("col"),
            P("col", "row"),
            P("col"),
            P(None, "col"),
            P(None, "col"),
        ),
        check_vma=False,
    )
```

time: 851 us -> 542 us (0.64)
  waiting for transfers between devices: 422 us -> 192 us
  blocking collectives: 107 us -> 17.4 us
  matrix products: 174 us -> 88.3 us
  starting transfers between devices: 2.2 us -> 83.3 us
  Pallas kernels: 0 us -> 49.7 us
  local copies, waits for them, and re-layouts: 60.1 us -> 45.1 us
  between operations: 16.3 us -> 2.61 us
    all_gather x12 -> x0, waiting for transfers between devices: 256 us -> none  [the longest x1 75.9 us: shards(): lax.all_gather(shrink_weight, 'row', axis=1, tiled=True)]
    ppermute x0 -> x71, waiting for transfers between devices: none -> 192 us  [peer(): return lax.ppermute(value, axis, [(i, i ^ p) for i in range(n)])]
    reduce_scatter x12 -> x0, waiting for transfers between devices: 160 us -> none  [the longest x1 65.7 us: shards(): lax.psum_scatter(expand_grad.astype(jnp.bfloat16), 'row', scatter_dimensi...]
    dot_general x36 -> x12, matrix products: 174 us -> 88.3 us  [the longest x1 14.8 us: shards(): jnp.einsum('itd,hd->ith', seed_low, shrink_full, preferred_element_type=F32)]
    psum x3 -> x0, blocking collectives: 85.3 us -> none  [the longest x1 78.3 us: shards(): lax.psum((heads_bias_grad, merge_bias_grad, expand_bias_grad, shrink_bias...]
    ppermute x0 -> x71, starting transfers between devices: none -> 83.3 us  [peer(): return lax.ppermute(value, axis, [(i, i ^ p) for i in range(n)])]
    pallas_call x0 -> x2, Pallas kernels: none -> 49.7 us  [the longest x1 29.8 us: attend_back(): pl.pallas_call(functools.partial(attend_back_kernel, length), grid=(count...]
    select_n x2 -> x32, other arithmetic: 0.01 us -> 16 us  [the longest x27 13.3 us: xor_order(): value = jnp.where(index & bit != 0, swapped, value)]
  transfers between devices with their start and end apart: 25 -> 71, of which waited for: 15 -> 25; matrix products, arithmetic and copies ran while one was open for 30% -> 33% of each run, Pallas kernels for 0% -> 9%
where the time goes in v1:
time: 542 us; the launch traced here: 537 us
  waiting for transfers between devices  192 us (35%)
  matrix products  88.3 us (16%)
  starting transfers between devices  83.3 us (15%)
  other arithmetic  58.1 us (11%)
  Pallas kernels  49.7 us (9%)
  local copies, waits for them, and re-layouts  45.1 us (8%)
  blocking collectives  17.4 us (3%)
    ppermute x71, waiting for transfers between devices, peer(): return lax.ppermute(value, axis, [(i, i ^ p) for i in range(n)])  192 us
    ppermute x71, starting transfers between devices, peer(): return lax.ppermute(value, axis, [(i, i ^ p) for i in range(n)])  83.3 us
    pallas_call x1, Pallas kernels, attend_back(): pl.pallas_call(functools.partial(attend_back_kernel, length), grid=(count...  29.8 us
    pallas_call x1, Pallas kernels, attend(): pl.pallas_call(functools.partial(attend_kernel, length), grid=(count, wid...  19.9 us
    unnamed x157, local copies, waits for them, and re-layouts  19.6 us
    psum x1, blocking collectives, shards(): totals = lax.psum(jnp.sum(member, axis=0), ('dp', 'row'))  17.4 us
    dot_general x1, matrix products, shards(): jnp.einsum('itd,hd->ith', seed_low, shrink_full, preferred_element_type=F32)  14.8 us
    dot_general x1, matrix products, shards(): jnp.einsum('itd,dh->ith', normed_two, expand_full, preferred_element_type...  13.7 us
  transfers between devices with their start and end apart: 71, of which 25 were waited for; matrix products, arithmetic and copies ran while one was open for 33% of the time, Pallas kernels for 9%

profile of v1, /device:TPU:0, one launch (start us, length us, event | category | flops | bytes accessed | tf_op | source)
XLA Modules:
  0.0 537.0 jit_solution(13699065901528055366)
XLA Ops:
  4.4 3.1 collective-permute-start.1
  7.5 2.6 collective-permute-start.2
  16.6 17.4 %psum.7 = s32[2]{0:T(128)S(1)} all-reduce(s32[2]{0:T(128)S(1)} %fusion.46), channel_id=1, replica_groups=mesh['dp'=4,'row'=4,'col'=2] {'dp','row'}, use_global_device_ids=true, to_apply=%region_5.6 | all-reduce | flops 2 | bytes 16 | tf_op jit(solution)/shard_map/psum | solution.py:297
  43.4 4.8 collective-permute-done.8
  49.3 4.9 collective-permute-done.9
  54.2 1.9 collective-permute-start.10
  56.8 3.5 collective-permute-done.10
  65.0 2.3 collective-permute-start.6
  72.3 7.6 %collective-permute-done.4 = bf16[3,768,128]{2,1,0:T(8,128)(2,1)S(1)} collective-permute-done((bf16[3,768,128]{2,1,0:T(8,128)(2,1)S(1)}, bf16[3,768,128]{2,1,0:T(8,128)(2,1)S(1)}, u32[]{:S(2)}, u32[]{:S(2)}) %collective-permute-start.4) | collective-permute-done | bytes 589856 | tf_op jit(solution)/shard_map/ppermute | solution.py:19
  80.7 12.3 %collective-permute-done.5 = bf16[3,768,128]{2,1,0:T(8,128)(2,1)S(1)} collective-permute-done((bf16[3,768,128]{2,1,0:T(8,128)(2,1)S(1)}, bf16[3,768,128]{2,1,0:T(8,128)(2,1)S(1)}, u32[]{:S(2)}, u32[]{:S(2)}) %collective-permute-start.5) | collective-permute-done | bytes 589856 | tf_op jit(solution)/shard_map/ppermute | solution.py:19
  93.0 2.5 collective-permute-start.13
  95.5 4.5 convolution_bitcast_fusion
  100.1 2.2 fusion.24
  103.4 19.9 %attend.1 = bf16[2,592,512]{2,1,0:T(8,128)(2,1)} custom-call(bf16[2,592,512]{2,1,0:T(8,128)(2,1)} %get-tuple-element.59.q_ref, bf16[2,592,512]{2,1,0:T(8,128)(2,1)} %fusion.31.k_ref, bf16[2,592,512]{2,1,0:T(8,128)(2,1)} %get-tuple-element.58.v_ref), custom_call_target="tpu_custom_call" | custom-call | flops 1435500544 | bytes 4849664 | tf_op jit(solution)/shard_map/attend/pallas_call | solution.py:157
  123.3 2.5 collective-permute-start.16
  125.8 1.9 collective-permute-start.17
  127.7 2.9 convolution_convert_fusion
  131.7 18.3 %collective-permute-done.16 = bf16[256,512]{1,0:T(8,128)(2,1)S(1)} collective-permute-done((bf16[256,512]{1,0:T(8,128)(2,1)}, bf16[256,512]{1,0:T(8,128)(2,1)S(1)}, u32[]{:S(2)}, u32[]{:S(2)}) %collective-permute-start.16) | collective-permute-done | bytes 262176 | tf_op jit(solution)/shard_map/ppermute | solution.py:19
  150.0 2.1 collective-permute-start.23
  152.5 14.3 %collective-permute-done.22 = bf16[512,256]{1,0:T(8,128)(2,1)S(1)} collective-permute-done((bf16[512,256]{1,0:T(8,128)(2,1)S(1)}, bf16[512,256]{1,0:T(8,128)(2,1)S(1)}, u32[]{:S(2)}, u32[]{:S(2)}) %collective-permute-start.22) | collective-permute-done | bytes 262176 | tf_op jit(solution)/shard_map/ppermute | solution.py:19
  177.8 40.3 %collective-permute-done.19 = bf16[768,512]{1,0:T(8,128)(2,1)S(1)} collective-permute-done((bf16[768,512]{1,0:T(8,128)(2,1)S(1)}, bf16[768,512]{1,0:T(8,128)(2,1)S(1)}, u32[]{:S(2)}, u32[]{:S(2)}) %collective-permute-start.19) | collective-permute-done | bytes 786464 | tf_op jit(solution)/shard_map/ppermute | solution.py:19
  219.3 13.7 %multiply_convert_fusion.1 = (bf16[2,592,2048]{2,1,0:T(8,128)(2,1)}, f32[2,592,2048]{2,1,0:T(8,128)}) fusion(f32[2048]{0:T(1024)S(1)} %fusion.39, bf16[768,512]{1,0:T(8,128)(2,1)} %copy-done.60, bf16[768,512]{1,0:T(8,128)(2,1)} %copy-done.58, bf16[768,512]{1,0:T(8,128)(2,1)} %copy-done.56, bf16[768,512]{1,0:T(8,128)(2,1)S(1)} %constant_dynamic-update-slice_fusion.6, ...), kind=kOutput, calls=%fused_computation.3 | convolution fusion | flops 5010063360 | bytes 23618816 | tf_op jit(solution)/shard_map/itd,dh->ith/dot_general | solution.py:313
  233.0 8.3 %bitcast_convert_fusion = bf16[2048,1024]{1,0:T(8,128)(2,1)S(1)} fusion(bf16[2,592,2048]{2,1,0:T(8,128)(2,1)} %get-tuple-element.208, bf16[2,592,1024]{2,1,0:T(8,128)(2,1)S(1)} %get-tuple-element.51), kind=kOutput, calls=%fused_computation.5 | convolution fusion | flops 4968153088 | bytes 11468800 | tf_op jit(solution)/shard_map/ith,itd->hd/dot_general | solution.py:322
  247.8 14.8 %convert_reduce_fusion = (f32[2048]{0:T(1024)S(1)}, bf16[2,592,2048]{2,1,0:T(8,128)(2,1)}) fusion(f32[2,592,2048]{2,1,0:T(8,128)} %get-tuple-element.209, f32[2048]{0:T(1024)S(1)} %fusion.39, bf16[2,592,1024]{2,1,0:T(8,128)(2,1)S(1)} %get-tuple-element.51, bf16[512,768]{1,0:T(8,128)(2,1)} %collective-permute-done.26, ...), kind=kOutput, calls=%fused_computation | convolution fusion | flops 5023397888 | bytes 21184512 | tf_op jit(solution)/shard_map/itd,hd->ith/dot_general | solution.py:324
  262.6 8.7 %bitcast_convert_fusion.1 = bf16[1024,2048]{1,0:T(8,128)(2,1)S(1)} fusion(bf16[2,592,2048]{2,1,0:T(8,128)(2,1)} %get-tuple-element.211, f32[2,592,1024]{2,1,0:T(8,128)S(1)} %get-tuple-element.55, f32[1024]{0:T(1024)S(1)} %bitcast.124, f32[1024]{0:T(1024)S(1)} %bitcast.105, f32[2,592]{1,0:T(2,128)S(1)} %add_rsqrt_fusion, ...), kind=kOutput, calls=%fused_computation.6 | convolution fusion | flops 4974215168 | bytes 13911296 | tf_op jit(solution)/shard_map/itd,ith->dh/dot_general | solution.py:328
  276.4 8.6 %convolution_convert_fusion.2 = bf16[2,592,1024]{2,1,0:T(8,128)(2,1)S(1)} fusion(bf16[2,592,2048]{2,1,0:T(8,128)(2,1)} %get-tuple-element.208, bf16[512,768]{1,0:T(8,128)(2,1)} %collective-permute-done.26, bf16[512,768]{1,0:T(8,128)(2,1)} %collective-permute-done.25, bf16[512,768]{1,0:T(8,128)(2,1)} %collective-permute-done.24, ...), kind=kOutput, calls=%fused_computation.80 | convolution fusion | flops 4988239872 | bytes 11468800 | tf_op jit(solution)/shard_map/ith,hd->itd/dot_general | solution.py:336
  286.7 10.7 %convolution_convert_fusion.1 = bf16[2,592,1024]{2,1,0:T(8,128)(2,1)S(1)} fusion(bf16[2,592,2048]{2,1,0:T(8,128)(2,1)} %get-tuple-element.211, bf16[768,512]{1,0:T(8,128)(2,1)} %copy-done.60, bf16[768,512]{1,0:T(8,128)(2,1)S(1)} %copy-done.59, bf16[768,512]{1,0:T(8,128)(2,1)S(1)} %copy-done.57, bf16[768,512]{1,0:T(8,128)(2,1)S(1)} %copy-done.35, ...), kind=kOutput, calls=%fused_computation.79 | convolution fusion | flops 4988239872 | bytes 11468800 | tf_op jit(solution)/shard_map/ith,dh->itd/dot_general | solution.py:326
  298.6 1.9 fusion.71
  302.5 3.1 add_convert_fusion.2
  305.7 2.5 collective-permute-start.66
  308.2 1.9 collective-permute-start.67
  310.1 13.6 %collective-permute-done.54 = bf16[1024,512]{1,0:T(8,128)(2,1)} collective-permute-done((bf16[1024,512]{1,0:T(8,128)(2,1)}, bf16[1024,512]{1,0:T(8,128)(2,1)}, u32[]{:S(2)}, u32[]{:S(2)}) %collective-permute-start.54) | collective-permute-done | bytes 1048608 | tf_op jit(solution)/shard_map/ppermute | solution.py:19
  323.7 2.4 add_convert_fusion.3
  326.2 2.6 collective-permute-start.57
  332.7 4.3 collective-permute-done.56
  337.1 7.0 %collective-permute-done.57 = bf16[256,512]{1,0:T(8,128)(2,1)S(1)} collective-permute-done((bf16[256,512]{1,0:T(8,128)(2,1)S(1)}, bf16[256,512]{1,0:T(8,128)(2,1)S(1)}, u32[]{:S(2)}, u32[]{:S(2)}) %collective-permute-start.57) | collective-permute-done | bytes 262176 | tf_op jit(solution)/shard_map/ppermute | solution.py:19
  345.8 2.0 collective-permute-start.60
  348.2 3.3 collective-permute-done.70
  351.9 3.1 collective-permute-done.60
  355.0 2.1 collective-permute-done.61
  360.8 2.5 multiply_reduce_fusion
  363.3 4.6 convert_reduce_fusion.3
  374.9 3.7 convolution_convert_fusion.3.up_ref
  378.6 29.8 %attend_back.1 = (bf16[2,592,512]{2,1,0:T(8,128)(2,1)}, bf16[2,592,512]{2,1,0:T(8,128)(2,1)}, bf16[2,592,512]{2,1,0:T(8,128)(2,1)}) custom-call(bf16[2,592,512]{2,1,0:T(8,128)(2,1)} %get-tuple-element.59.q_ref, bf16[2,592,512]{2,1,0:T(8,128)(2,1)} %fusion.31.k_ref, bf16[2,592,512]{2,1,0:T(8,128)(2,1)} %get-tuple-element.58.v_ref, ...), custom_call_target="tpu_custom_call" | custom-call | flops 3588751360 | bytes 8486912 | tf_op jit(solution)/shard_map/attend_back/pallas_call | solution.py:221
  408.6 6.9 %fusion.21 = bf16[3,1024,512]{2,1,0:T(8,128)(2,1)S(1)} fusion(bf16[1,2,592,512]{3,2,1,0:T(8,128)(2,1)} %bitcast.94, bf16[1,2,592,512]{3,2,1,0:T(8,128)(2,1)} %bitcast.125, bf16[1,2,592,512]{3,2,1,0:T(8,128)(2,1)} %bitcast.96, bf16[2,592,1024]{2,1,0:T(8,128)(2,1)S(1)} %get-tuple-element.57, f32[1024]{0:T(1024)S(1)} %bitcast.122, f32[1024]{0:T(1024)S(1)} %bitcast.99, ...), kind=kOutput, calls=%fused_computation.51 | convolution fusion | flops 3737026560 | bytes 9225472 | tf_op jit(solution)/shard_map/itd,kitf->kdf/dot_general | solution.py:348
  415.5 4.0 bitcast_convert_fusion.3
  425.9 2.4 fusion.29
  430.2 4.0 collective-permute-start.47
  434.7 2.0 collective-permute-start.49
  438.5 3.8 collective-permute-done.48
  445.4 18.1 %collective-permute-done.50 = bf16[128,256]{1,0:T(8,128)(2,1)S(1)} collective-permute-done((bf16[128,256]{1,0:T(8,128)(2,1)S(1)}, bf16[128,256]{1,0:T(8,128)(2,1)S(1)}, u32[]{:S(2)}, u32[]{:S(2)}) %collective-permute-start.50) | collective-permute-done | bytes 65568 | tf_op jit(solution)/shard_map/ppermute | solution.py:19
  464.3 4.4 collective-permute-done.51
  469.3 1.9 copy.35
  471.2 4.3 collective-permute-done.52
  479.6 2.0 collective-permute-start.36
  481.6 5.4 %collective-permute-done.34 = bf16[3,256,128]{2,1,0:T(8,128)(2,1)S(1)} collective-permute-done((bf16[3,256,128]{2,1,0:T(8,128)(2,1)S(1)}, bf16[3,256,128]{2,1,0:T(8,128)(2,1)S(1)}, u32[]{:S(2)}, u32[]{:S(2)}) %collective-permute-start.34) | collective-permute-done | bytes 196640 | tf_op jit(solution)/shard_map/ppermute | solution.py:19
  487.1 7.1 %collective-permute-done.35 = bf16[3,256,128]{2,1,0:T(8,128)(2,1)S(1)} collective-permute-done((bf16[3,256,128]{2,1,0:T(8,128)(2,1)S(1)}, bf16[3,256,128]{2,1,0:T(8,128)(2,1)S(1)}, u32[]{:S(2)}, u32[]{:S(2)}) %collective-permute-start.35) | collective-permute-done | bytes 196640 | tf_op jit(solution)/shard_map/ppermute | solution.py:19
  500.1 3.2 collective-permute-done.38
  503.3 1.9 collective-permute-done.39
  507.0 2.6 fusion.12
  511.6 4.9 fusion.11
  520.1 2.1 collective-permute-done.41
  522.3 4.0 collective-permute-start.42
  530.5 3.2 copy.36
  (398 shorter events, 119.1 us)
Async XLA Ops:
  4.4 56.5 %collective-permute-start.1 = (bf16[3,256,128]{2,1,0:T(8,128)(2,1)}, bf16[3,256,128]{2,1,0:T(8,128)(2,1)}, u32[]{:S(2)}, u32[]{:S(2)}) collective-permute-start(bf16[3,256,128]{2,1,0:T(8,128)(2,1)} %slice.699), channel_id=1, source_target_pairs={{0,2},{2,0},{4,6},{6,4},{1,3},{3,1},{5,7},{7,5},{8,10},{10,8},{12,... | collective-permute-start | bytes 589832 | tf_op jit(solution)/shard_map/ppermute | solution.py:19
  7.5 54.3 %collective-permute-start.2 = (bf16[3,256,128]{2,1,0:T(8,128)(2,1)}, bf16[3,256,128]{2,1,0:T(8,128)(2,1)}, u32[]{:S(2)}, u32[]{:S(2)}) collective-permute-start(bf16[3,256,128]{2,1,0:T(8,128)(2,1)} %slice.699), channel_id=1, source_target_pairs={{0,4},{2,6},{4,0},{6,2},{1,5},{3,7},{5,1},{7,3},{8,12},{10,14},{12... | collective-permute-start | bytes 589832 | tf_op jit(solution)/shard_map/ppermute | solution.py:19
  10.1 52.7 %collective-permute-start.3 = (bf16[3,256,128]{2,1,0:T(8,128)(2,1)}, bf16[3,256,128]{2,1,0:T(8,128)(2,1)}, u32[]{:S(2)}, u32[]{:S(2)}) collective-permute-start(bf16[3,256,128]{2,1,0:T(8,128)(2,1)} %slice.699), channel_id=1, source_target_pairs={{0,6},{2,4},{4,2},{6,0},{1,7},{3,5},{5,3},{7,1},{8,14},{10,12},{12... | collective-permute-start | bytes 589832 | tf_op jit(solution)/shard_map/ppermute | solution.py:19
  12.7 52.4 %collective-permute-start = (bf16[2,592,512]{2,1,0:T(8,128)(2,1)}, bf16[2,592,512]{2,1,0:T(8,128)(2,1)}, u32[]{:S(2)}, u32[]{:S(2)}) collective-permute-start(bf16[2,592,512]{2,1,0:T(8,128)(2,1)} %pad.7), channel_id=1, source_target_pairs={{0,1},{1,0},{2,3},{3,2},{4,5},{5,4},{6,7},{7,6},{8,9},{9,8},{10,11... | collective-permute-start | bytes 3637256 | tf_op jit(solution)/shard_map/ppermute | solution.py:19
  12.8 30.5 %collective-permute-start.7 = (bf16[6,512]{1,0:T(8,128)(2,1)S(1)}, bf16[6,512]{1,0:T(8,128)(2,1)S(1)}, u32[]{:S(2)}, u32[]{:S(2)}) collective-permute-start(bf16[6,512]{1,0:T(8,128)(2,1)S(1)} %pad_maximum_fusion.4), channel_id=1, source_target_pairs={{0,1},{1,0},{2,3},{3,2},{4,5},{5,4},{6,7},{7,6},{8,9},{9,8},{10,11... | collective-permute-start | bytes 18440 | tf_op jit(solution)/shard_map/ppermute | solution.py:19
  54.2 6.1 %collective-permute-start.10 = (bf16[128,256]{1,0:T(8,128)(2,1)S(1)}, bf16[128,256]{1,0:T(8,128)(2,1)S(1)}, u32[]{:S(2)}, u32[]{:S(2)}) collective-permute-start(bf16[128,256]{1,0:T(8,128)(2,1)S(1)} %slice.717), channel_id=1, source_target_pairs={{0,6},{2,4},{4,2},{6,0},{1,7},{3,5},{5,3},{7,1},{8,14},{10,12},{12... | collective-permute-start | bytes 196616 | tf_op jit(solution)/shard_map/ppermute | solution.py:19
  60.2 70.4 %collective-permute-start.15 = (bf16[256,512]{1,0:T(8,128)(2,1)}, bf16[256,512]{1,0:T(8,128)(2,1)}, u32[]{:S(2)}, u32[]{:S(2)}) collective-permute-start(bf16[256,512]{1,0:T(8,128)(2,1)} %slice.731), channel_id=1, source_target_pairs={{0,2},{2,0},{4,6},{6,4},{1,3},{3,1},{5,7},{7,5},{8,10},{10,8},{12,... | collective-permute-start | bytes 786440 | tf_op jit(solution)/shard_map/ppermute | solution.py:19
  60.9 107.9 %collective-permute-start.28 = (bf16[2,592,512]{2,1,0:T(8,128)(2,1)S(1)}, bf16[2,592,512]{2,1,0:T(8,128)(2,1)S(1)}, u32[]{:S(2)}, u32[]{:S(2)}) collective-permute-start(bf16[2,592,512]{2,1,0:T(8,128)(2,1)S(1)} %pad.8), channel_id=1, source_target_pairs={{0,1},{1,0},{2,3},{3,2},{4,5},{5,4},{6,7},{7,6},{8,9},{9,8},{10,11... | collective-permute-start | bytes 3637256 | tf_op jit(solution)/shard_map/ppermute | solution.py:19
  63.8 16.2 %collective-permute-start.4 = (bf16[3,768,128]{2,1,0:T(8,128)(2,1)S(1)}, bf16[3,768,128]{2,1,0:T(8,128)(2,1)S(1)}, u32[]{:S(2)}, u32[]{:S(2)}) collective-permute-start(bf16[3,768,128]{2,1,0:T(8,128)(2,1)S(1)} %constant_dynamic-update-slice_fusion), channel_id=1, source_target_pairs={{0,8},{8,0},{16,24},{24,16},{1,9},{9,1},{17,25},{25,17},{2,10},{10... | collective-permute-start | bytes 1769480 | tf_op jit(solution)/shard_map/ppermute | solution.py:19
  64.5 28.4 %collective-permute-start.5 = (bf16[3,768,128]{2,1,0:T(8,128)(2,1)S(1)}, bf16[3,768,128]{2,1,0:T(8,128)(2,1)S(1)}, u32[]{:S(2)}, u32[]{:S(2)}) collective-permute-start(bf16[3,768,128]{2,1,0:T(8,128)(2,1)S(1)} %constant_dynamic-update-slice_fusion), channel_id=1, source_target_pairs={{0,16},{8,24},{16,0},{24,8},{1,17},{9,25},{17,1},{25,9},{2,18},{10... | collective-permute-start | bytes 1769480 | tf_op jit(solution)/shard_map/ppermute | solution.py:19
  65.0 27.9 %collective-permute-start.6 = (bf16[3,768,128]{2,1,0:T(8,128)(2,1)S(1)}, bf16[3,768,128]{2,1,0:T(8,128)(2,1)S(1)}, u32[]{:S(2)}, u32[]{:S(2)}) collective-permute-start(bf16[3,768,128]{2,1,0:T(8,128)(2,1)S(1)} %constant_dynamic-update-slice_fusion), channel_id=1, source_target_pairs={{0,24},{8,16},{16,8},{24,0},{1,25},{9,17},{17,9},{25,1},{2,26},{10... | collective-permute-start | bytes 1769480 | tf_op jit(solution)/shard_map/ppermute | solution.py:19
  80.0 43.4 %collective-permute-start.11 = (bf16[128,768]{1,0:T(8,128)(2,1)}, bf16[128,768]{1,0:T(8,128)(2,1)}, u32[]{:S(2)}, u32[]{:S(2)}) collective-permute-start(bf16[128,768]{1,0:T(8,128)(2,1)} %constant_dynamic-update-slice_fusion.3), channel_id=1, source_target_pairs={{0,8},{8,0},{16,24},{24,16},{1,9},{9,1},{17,25},{25,17},{2,10},{10... | collective-permute-start | bytes 589832 | tf_op jit(solution)/shard_map/ppermute | solution.py:19
  92.9 32.9 %collective-permute-start.12 = (bf16[128,768]{1,0:T(8,128)(2,1)}, bf16[128,768]{1,0:T(8,128)(2,1)}, u32[]{:S(2)}, u32[]{:S(2)}) collective-permute-start(bf16[128,768]{1,0:T(8,128)(2,1)} %constant_dynamic-update-slice_fusion.3), channel_id=1, source_target_pairs={{0,16},{8,24},{16,0},{24,8},{1,17},{9,25},{17,1},{25,9},{2,18},{10... | collective-permute-start | bytes 589832 | tf_op jit(solution)/shard_map/ppermute | solution.py:19
  93.0 34.7 %collective-permute-start.13 = (bf16[128,768]{1,0:T(8,128)(2,1)}, bf16[128,768]{1,0:T(8,128)(2,1)}, u32[]{:S(2)}, u32[]{:S(2)}) collective-permute-start(bf16[128,768]{1,0:T(8,128)(2,1)} %constant_dynamic-update-slice_fusion.3), channel_id=1, source_target_pairs={{0,24},{8,16},{16,8},{24,0},{1,25},{9,17},{17,9},{25,1},{2,26},{10... | collective-permute-start | bytes 589832 | tf_op jit(solution)/shard_map/ppermute | solution.py:19
  123.3 26.6 %collective-permute-start.16 = (bf16[256,512]{1,0:T(8,128)(2,1)}, bf16[256,512]{1,0:T(8,128)(2,1)S(1)}, u32[]{:S(2)}, u32[]{:S(2)}) collective-permute-start(bf16[256,512]{1,0:T(8,128)(2,1)} %slice.731), channel_id=1, source_target_pairs={{0,4},{2,6},{4,0},{6,2},{1,5},{3,7},{5,1},{7,3},{8,12},{10,14},{12... | collective-permute-start | bytes 786440 | tf_op jit(solution)/shard_map/ppermute | solution.py:19
  125.8 24.2 %collective-permute-start.17 = (bf16[256,512]{1,0:T(8,128)(2,1)}, bf16[256,512]{1,0:T(8,128)(2,1)S(1)}, u32[]{:S(2)}, u32[]{:S(2)}) collective-permute-start(bf16[256,512]{1,0:T(8,128)(2,1)} %slice.731), channel_id=1, source_target_pairs={{0,6},{2,4},{4,2},{6,0},{1,7},{3,5},{5,3},{7,1},{8,14},{10,12},{12... | collective-permute-start | bytes 786440 | tf_op jit(solution)/shard_map/ppermute | solution.py:19
  127.7 24.4 %collective-permute-start.21 = (bf16[512,256]{1,0:T(8,128)(2,1)S(1)}, bf16[512,256]{1,0:T(8,128)(2,1)S(1)}, u32[]{:S(2)}, u32[]{:S(2)}) collective-permute-start(bf16[512,256]{1,0:T(8,128)(2,1)S(1)} %copy-done.33), channel_id=1, source_target_pairs={{0,2},{2,0},{4,6},{6,4},{1,3},{3,1},{5,7},{7,5},{8,10},{10,8},{12,... | collective-permute-start | bytes 786440 | tf_op jit(solution)/shard_map/ppermute | solution.py:19
  130.6 43.4 %collective-permute-start.14 = (bf16[2,592,1024]{2,1,0:T(8,128)(2,1)S(1)}, bf16[2,592,1024]{2,1,0:T(8,128)(2,1)S(1)}, u32[]{:S(2)}, u32[]{:S(2)}) collective-permute-start(bf16[2,592,1024]{2,1,0:T(8,128)(2,1)S(1)} %convolution_convert_fusion), channel_id=1, source_target_pairs={{0,1},{1,0},{2,3},{3,2},{4,5},{5,4},{6,7},{7,6},{8,9},{9,8},{10,11... | collective-permute-start | bytes 7274504 | tf_op jit(solution)/shard_map/ppermute | solution.py:19
  150.0 16.9 %collective-permute-start.22 = (bf16[512,256]{1,0:T(8,128)(2,1)S(1)}, bf16[512,256]{1,0:T(8,128)(2,1)S(1)}, u32[]{:S(2)}, u32[]{:S(2)}) collective-permute-start(bf16[512,256]{1,0:T(8,128)(2,1)S(1)} %copy-done.33), channel_id=1, source_target_pairs={{0,4},{2,6},{4,0},{6,2},{1,5},{3,7},{5,1},{7,3},{8,12},{10,14},{12... | collective-permute-start | bytes 786440 | tf_op jit(solution)/shard_map/ppermute | solution.py:19
  150.0 17.2 %collective-permute-start.23 = (bf16[512,256]{1,0:T(8,128)(2,1)S(1)}, bf16[512,256]{1,0:T(8,128)(2,1)S(1)}, u32[]{:S(2)}, u32[]{:S(2)}) collective-permute-start(bf16[512,256]{1,0:T(8,128)(2,1)S(1)} %copy-done.33), channel_id=1, source_target_pairs={{0,6},{2,4},{4,2},{6,0},{1,7},{3,5},{5,3},{7,1},{8,14},{10,12},{12... | collective-permute-start | bytes 786440 | tf_op jit(solution)/shard_map/ppermute | solution.py:19
  152.1 24.1 %collective-permute-start.18 = (bf16[768,512]{1,0:T(8,128)(2,1)S(1)}, bf16[768,512]{1,0:T(8,128)(2,1)S(1)}, u32[]{:S(2)}, u32[]{:S(2)}) collective-permute-start(bf16[768,512]{1,0:T(8,128)(2,1)S(1)} %constant_dynamic-update-slice_fusion.6), channel_id=1, source_target_pairs={{0,8},{8,0},{16,24},{24,16},{1,9},{9,1},{17,25},{25,17},{2,10},{10... | collective-permute-start | bytes 2359304 | tf_op jit(solution)/shard_map/ppermute | solution.py:19
  166.8 51.3 %collective-permute-start.19 = (bf16[768,512]{1,0:T(8,128)(2,1)S(1)}, bf16[768,512]{1,0:T(8,128)(2,1)S(1)}, u32[]{:S(2)}, u32[]{:S(2)}) collective-permute-start(bf16[768,512]{1,0:T(8,128)(2,1)S(1)} %constant_dynamic-update-slice_fusion.6), channel_id=1, source_target_pairs={{0,16},{8,24},{16,0},{24,8},{1,17},{9,25},{17,1},{25,9},{2,18},{10... | collective-permute-start | bytes 2359304 | tf_op jit(solution)/shard_map/ppermute | solution.py:19
  167.2 50.9 %collective-permute-start.20 = (bf16[768,512]{1,0:T(8,128)(2,1)S(1)}, bf16[768,512]{1,0:T(8,128)(2,1)S(1)}, u32[]{:S(2)}, u32[]{:S(2)}) collective-permute-start(bf16[768,512]{1,0:T(8,128)(2,1)S(1)} %constant_dynamic-update-slice_fusion.6), channel_id=1, source_target_pairs={{0,24},{8,16},{16,8},{24,0},{1,25},{9,17},{17,9},{25,1},{2,26},{10... | collective-permute-start | bytes 2359304 | tf_op jit(solution)/shard_map/ppermute | solution.py:19
  168.8 77.6 %collective-permute-start.24 = (bf16[512,768]{1,0:T(8,128)(2,1)S(1)}, bf16[512,768]{1,0:T(8,128)(2,1)}, u32[]{:S(2)}, u32[]{:S(2)}) collective-permute-start(bf16[512,768]{1,0:T(8,128)(2,1)S(1)} %constant_dynamic-update-slice_fusion.9), channel_id=1, source_target_pairs={{0,8},{8,0},{16,24},{24,16},{1,9},{9,1},{17,25},{25,17},{2,10},{10... | collective-permute-start | bytes 2359304 | tf_op jit(solution)/shard_map/ppermute | solution.py:19
  174.0 73.8 %collective-permute-start.25 = (bf16[512,768]{1,0:T(8,128)(2,1)S(1)}, bf16[512,768]{1,0:T(8,128)(2,1)}, u32[]{:S(2)}, u32[]{:S(2)}) collective-permute-start(bf16[512,768]{1,0:T(8,128)(2,1)S(1)} %constant_dynamic-update-slice_fusion.9), channel_id=1, source_target_pairs={{0,16},{8,24},{16,0},{24,8},{1,17},{9,25},{17,1},{25,9},{2,18},{10... | collective-permute-start | bytes 2359304 | tf_op jit(solution)/shard_map/ppermute | solution.py:19
  176.3 71.6 %collective-permute-start.26 = (bf16[512,768]{1,0:T(8,128)(2,1)S(1)}, bf16[512,768]{1,0:T(8,128)(2,1)}, u32[]{:S(2)}, u32[]{:S(2)}) collective-permute-start(bf16[512,768]{1,0:T(8,128)(2,1)S(1)} %constant_dynamic-update-slice_fusion.9), channel_id=1, source_target_pairs={{0,24},{8,16},{16,8},{24,0},{1,25},{9,17},{17,9},{25,1},{2,26},{10... | collective-permute-start | bytes 2359304 | tf_op jit(solution)/shard_map/ppermute | solution.py:19
  244.3 56.2 %collective-permute-start.62 = (bf16[512,1024]{1,0:T(8,128)(2,1)}, bf16[512,1024]{1,0:T(8,128)(2,1)}, u32[]{:S(2)}, u32[]{:S(2)}) collective-permute-start(bf16[512,1024]{1,0:T(8,128)(2,1)} %get-tuple-element.77), channel_id=1, source_target_pairs={{0,8},{8,0},{16,24},{24,16},{1,9},{9,1},{17,25},{25,17},{2,10},{10... | collective-permute-start | bytes 3145736 | tf_op jit(solution)/shard_map/ppermute | solution.py:19
  244.8 57.6 %collective-permute-start.63 = (bf16[512,1024]{1,0:T(8,128)(2,1)}, bf16[512,1024]{1,0:T(8,128)(2,1)}, u32[]{:S(2)}, u32[]{:S(2)}) collective-permute-start(bf16[512,1024]{1,0:T(8,128)(2,1)} %get-tuple-element.79), channel_id=1, source_target_pairs={{0,16},{8,24},{16,0},{24,8},{1,17},{9,25},{17,1},{25,9},{2,18},{10... | collective-permute-start | bytes 3145736 | tf_op jit(solution)/shard_map/ppermute | solution.py:19
  246.4 56.1 %collective-permute-start.64 = (bf16[512,1024]{1,0:T(8,128)(2,1)}, bf16[512,1024]{1,0:T(8,128)(2,1)}, u32[]{:S(2)}, u32[]{:S(2)}) collective-permute-start(bf16[512,1024]{1,0:T(8,128)(2,1)} %get-tuple-element.78), channel_id=1, source_target_pairs={{0,24},{8,16},{16,8},{24,0},{1,25},{9,17},{17,9},{25,1},{2,26},{10... | collective-permute-start | bytes 3145736 | tf_op jit(solution)/shard_map/ppermute | solution.py:19
  274.4 33.9 %collective-permute-start.53 = (bf16[1024,512]{1,0:T(8,128)(2,1)}, bf16[1024,512]{1,0:T(8,128)(2,1)}, u32[]{:S(2)}, u32[]{:S(2)}) collective-permute-start(bf16[1024,512]{1,0:T(8,128)(2,1)} %get-tuple-element.80), channel_id=1, source_target_pairs={{0,8},{8,0},{16,24},{24,16},{1,9},{9,1},{17,25},{25,17},{2,10},{10... | collective-permute-start | bytes 3145736 | tf_op jit(solution)/shard_map/ppermute | solution.py:19
  274.9 48.8 %collective-permute-start.54 = (bf16[1024,512]{1,0:T(8,128)(2,1)}, bf16[1024,512]{1,0:T(8,128)(2,1)}, u32[]{:S(2)}, u32[]{:S(2)}) collective-permute-start(bf16[1024,512]{1,0:T(8,128)(2,1)} %get-tuple-element.82), channel_id=1, source_target_pairs={{0,16},{8,24},{16,0},{24,8},{1,17},{9,25},{17,1},{25,9},{2,18},{10... | collective-permute-start | bytes 3145736 | tf_op jit(solution)/shard_map/ppermute | solution.py:19
  300.6 23.1 %collective-permute-start.55 = (bf16[1024,512]{1,0:T(8,128)(2,1)}, bf16[1024,512]{1,0:T(8,128)(2,1)S(1)}, u32[]{:S(2)}, u32[]{:S(2)}) collective-permute-start(bf16[1024,512]{1,0:T(8,128)(2,1)} %get-tuple-element.81), channel_id=1, source_target_pairs={{0,24},{8,16},{16,8},{24,0},{1,25},{9,17},{17,9},{25,1},{2,26},{10... | collective-permute-start | bytes 3145736 | tf_op jit(solution)/shard_map/ppermute | solution.py:19
  305.6 23.2 %collective-permute-start.65 = (bf16[512,256]{1,0:T(8,128)(2,1)S(1)}, bf16[512,256]{1,0:T(8,128)(2,1)S(1)}, u32[]{:S(2)}, u32[]{:S(2)}) collective-permute-start(bf16[512,256]{1,0:T(8,128)(2,1)S(1)} %get-tuple-element.113), channel_id=1, source_target_pairs={{0,2},{2,0},{4,6},{6,4},{1,3},{3,1},{5,7},{7,5},{8,10},{10,8},{12,... | collective-permute-start | bytes 786440 | tf_op jit(solution)/shard_map/ppermute | solution.py:19
  305.7 24.9 %collective-permute-start.66 = (bf16[512,256]{1,0:T(8,128)(2,1)S(1)}, bf16[512,256]{1,0:T(8,128)(2,1)S(1)}, u32[]{:S(2)}, u32[]{:S(2)}) collective-permute-start(bf16[512,256]{1,0:T(8,128)(2,1)S(1)} %get-tuple-element.115), channel_id=1, source_target_pairs={{0,4},{2,6},{4,0},{6,2},{1,5},{3,7},{5,1},{7,3},{8,12},{10,14},{12... | collective-permute-start | bytes 786440 | tf_op jit(solution)/shard_map/ppermute | solution.py:19
  308.2 22.4 %collective-permute-start.67 = (bf16[512,256]{1,0:T(8,128)(2,1)S(1)}, bf16[512,256]{1,0:T(8,128)(2,1)S(1)}, u32[]{:S(2)}, u32[]{:S(2)}) collective-permute-start(bf16[512,256]{1,0:T(8,128)(2,1)S(1)} %get-tuple-element.114), channel_id=1, source_target_pairs={{0,6},{2,4},{4,2},{6,0},{1,7},{3,5},{5,3},{7,1},{8,14},{10,12},{12... | collective-permute-start | bytes 786440 | tf_op jit(solution)/shard_map/ppermute | solution.py:19
  326.2 10.9 %collective-permute-start.56 = (bf16[256,512]{1,0:T(8,128)(2,1)S(1)}, bf16[256,512]{1,0:T(8,128)(2,1)S(1)}, u32[]{:S(2)}, u32[]{:S(2)}) collective-permute-start(bf16[256,512]{1,0:T(8,128)(2,1)S(1)} %get-tuple-element.118), channel_id=1, source_target_pairs={{0,2},{2,0},{4,6},{6,4},{1,3},{3,1},{5,7},{7,5},{8,10},{10,8},{12,... | collective-permute-start | bytes 786440 | tf_op jit(solution)/shard_map/ppermute | solution.py:19
  326.2 17.8 %collective-permute-start.57 = (bf16[256,512]{1,0:T(8,128)(2,1)S(1)}, bf16[256,512]{1,0:T(8,128)(2,1)S(1)}, u32[]{:S(2)}, u32[]{:S(2)}) collective-permute-start(bf16[256,512]{1,0:T(8,128)(2,1)S(1)} %get-tuple-element.120), channel_id=1, source_target_pairs={{0,4},{2,6},{4,0},{6,2},{1,5},{3,7},{5,1},{7,3},{8,12},{10,14},{12... | collective-permute-start | bytes 786440 | tf_op jit(solution)/shard_map/ppermute | solution.py:19
  328.8 15.6 %collective-permute-start.58 = (bf16[256,512]{1,0:T(8,128)(2,1)S(1)}, bf16[256,512]{1,0:T(8,128)(2,1)S(1)}, u32[]{:S(2)}, u32[]{:S(2)}) collective-permute-start(bf16[256,512]{1,0:T(8,128)(2,1)S(1)} %get-tuple-element.119), channel_id=1, source_target_pairs={{0,6},{2,4},{4,2},{6,0},{1,7},{3,5},{5,3},{7,1},{8,14},{10,12},{12... | collective-permute-start | bytes 786440 | tf_op jit(solution)/shard_map/ppermute | solution.py:19
  330.8 15.0 %collective-permute-start.68 = (bf16[512,256]{1,0:T(8,128)(2,1)S(1)}, bf16[512,256]{1,0:T(8,128)(2,1)S(1)}, u32[]{:S(2)}, u32[]{:S(2)}) collective-permute-start(bf16[512,256]{1,0:T(8,128)(2,1)S(1)} %add_convert_fusion.5), channel_id=1, source_target_pairs={{0,8},{8,0},{16,24},{24,16},{1,9},{9,1},{17,25},{25,17},{2,10},{10... | collective-permute-start | bytes 786440 | tf_op jit(solution)/shard_map/ppermute | solution.py:19
  331.3 16.5 %collective-permute-start.69 = (bf16[512,256]{1,0:T(8,128)(2,1)S(1)}, bf16[512,256]{1,0:T(8,128)(2,1)S(1)}, u32[]{:S(2)}, u32[]{:S(2)}) collective-permute-start(bf16[512,256]{1,0:T(8,128)(2,1)S(1)} %add_convert_fusion.5), channel_id=1, source_target_pairs={{0,24},{8,16},{16,8},{24,0},{1,25},{9,17},{17,9},{25,1},{2,26},{10... | collective-permute-start | bytes 786440 | tf_op jit(solution)/shard_map/ppermute | solution.py:19
  337.1 23.7 %collective-permute-start.29 = (bf16[2,592,1024]{2,1,0:T(8,128)(2,1)S(1)}, bf16[2,592,1024]{2,1,0:T(8,128)(2,1)S(1)}, u32[]{:S(2)}, u32[]{:S(2)}) collective-permute-start(bf16[2,592,1024]{2,1,0:T(8,128)(2,1)S(1)} %convolution_convert_fusion.1), channel_id=1, source_target_pairs={{0,1},{1,0},{2,3},{3,2},{4,5},{5,4},{6,7},{7,6},{8,9},{9,8},{10,11... | collective-permute-start | bytes 7274504 | tf_op jit(solution)/shard_map/ppermute | solution.py:19
  344.0 7.4 %collective-permute-start.70 = (bf16[512,256]{1,0:T(8,128)(2,1)S(1)}, bf16[512,256]{1,0:T(8,128)(2,1)S(1)}, u32[]{:S(2)}, u32[]{:S(2)}) collective-permute-start(bf16[512,256]{1,0:T(8,128)(2,1)S(1)} %add_convert_fusion.5), channel_id=1, source_target_pairs={{0,16},{8,24},{16,0},{24,8},{1,17},{9,25},{17,1},{25,9},{2,18},{10... | collective-permute-start | bytes 786440 | tf_op jit(solution)/shard_map/ppermute | solution.py:19
  344.6 7.3 %collective-permute-start.59 = (bf16[256,512]{1,0:T(8,128)(2,1)S(1)}, bf16[256,512]{1,0:T(8,128)(2,1)S(1)}, u32[]{:S(2)}, u32[]{:S(2)}) collective-permute-start(bf16[256,512]{1,0:T(8,128)(2,1)S(1)} %add_convert_fusion.6), channel_id=1, source_target_pairs={{0,8},{8,0},{16,24},{24,16},{1,9},{9,1},{17,25},{25,17},{2,10},{10... | collective-permute-start | bytes 786440 | tf_op jit(solution)/shard_map/ppermute | solution.py:19
  345.8 9.2 %collective-permute-start.60 = (bf16[256,512]{1,0:T(8,128)(2,1)S(1)}, bf16[256,512]{1,0:T(8,128)(2,1)S(1)}, u32[]{:S(2)}, u32[]{:S(2)}) collective-permute-start(bf16[256,512]{1,0:T(8,128)(2,1)S(1)} %add_convert_fusion.6), channel_id=1, source_target_pairs={{0,24},{8,16},{16,8},{24,0},{1,25},{9,17},{17,9},{25,1},{2,26},{10... | collective-permute-start | bytes 786440 | tf_op jit(solution)/shard_map/ppermute | solution.py:19
  347.7 9.3 %collective-permute-start.61 = (bf16[256,512]{1,0:T(8,128)(2,1)S(1)}, bf16[256,512]{1,0:T(8,128)(2,1)S(1)}, u32[]{:S(2)}, u32[]{:S(2)}) collective-permute-start(bf16[256,512]{1,0:T(8,128)(2,1)S(1)} %add_convert_fusion.6), channel_id=1, source_target_pairs={{0,16},{8,24},{16,0},{24,8},{1,17},{9,25},{17,1},{25,9},{2,18},{10... | collective-permute-start | bytes 786440 | tf_op jit(solution)/shard_map/ppermute | solution.py:19
  351.5 72.6 %collective-permute-start.27 = (bf16[2,592,512]{2,1,0:T(8,128)(2,1)}, bf16[2,592,512]{2,1,0:T(8,128)(2,1)}, u32[]{:S(2)}, u32[]{:S(2)}) collective-permute-start(bf16[2,592,512]{2,1,0:T(8,128)(2,1)} %get-tuple-element.89), channel_id=1, source_target_pairs={{0,1},{1,0},{2,3},{3,2},{4,5},{5,4},{6,7},{7,6},{8,9},{9,8},{10,11... | collective-permute-start | bytes 3637256 | tf_op jit(solution)/shard_map/ppermute | solution.py:19
  371.4 57.6 %collective-permute-start.44 = (bf16[128,1024]{1,0:T(8,128)(2,1)}, bf16[128,1024]{1,0:T(8,128)(2,1)S(1)}, u32[]{:S(2)}, u32[]{:S(2)}) collective-permute-start(bf16[128,1024]{1,0:T(8,128)(2,1)} %get-tuple-element.121), channel_id=1, source_target_pairs={{0,8},{8,0},{16,24},{24,16},{1,9},{9,1},{17,25},{25,17},{2,10},{10... | collective-permute-start | bytes 786440 | tf_op jit(solution)/shard_map/ppermute | solution.py:19
  372.8 56.2 %collective-permute-start.45 = (bf16[128,1024]{1,0:T(8,128)(2,1)}, bf16[128,1024]{1,0:T(8,128)(2,1)S(1)}, u32[]{:S(2)}, u32[]{:S(2)}) collective-permute-start(bf16[128,1024]{1,0:T(8,128)(2,1)} %get-tuple-element.123), channel_id=1, source_target_pairs={{0,16},{8,24},{16,0},{24,8},{1,17},{9,25},{17,1},{25,9},{2,18},{10... | collective-permute-start | bytes 786440 | tf_op jit(solution)/shard_map/ppermute | solution.py:19
  373.1 55.9 %collective-permute-start.46 = (bf16[128,1024]{1,0:T(8,128)(2,1)}, bf16[128,1024]{1,0:T(8,128)(2,1)}, u32[]{:S(2)}, u32[]{:S(2)}) collective-permute-start(bf16[128,1024]{1,0:T(8,128)(2,1)} %get-tuple-element.122), channel_id=1, source_target_pairs={{0,24},{8,16},{16,8},{24,0},{1,25},{9,17},{17,9},{25,1},{2,26},{10... | collective-permute-start | bytes 786440 | tf_op jit(solution)/shard_map/ppermute | solution.py:19
  419.6 87.4 %collective-permute-start.30 = (bf16[2,592,1024]{2,1,0:T(8,128)(2,1)S(1)}, bf16[2,592,1024]{2,1,0:T(8,128)(2,1)S(1)}, u32[]{:S(2)}, u32[]{:S(2)}) collective-permute-start(bf16[2,592,1024]{2,1,0:T(8,128)(2,1)S(1)} %bitcast_convert_fusion.3), channel_id=1, source_target_pairs={{0,1},{1,0},{2,3},{3,2},{4,5},{5,4},{6,7},{7,6},{8,9},{9,8},{10,11... | collective-permute-start | bytes 7274504 | tf_op jit(solution)/shard_map/ppermute | solution.py:19
  424.5 51.1 %collective-permute-start.31 = (bf16[3,1024,128]{2,1,0:T(8,128)(2,1)S(1)}, bf16[3,1024,128]{2,1,0:T(8,128)(2,1)S(1)}, u32[]{:S(2)}, u32[]{:S(2)}) collective-permute-start(bf16[3,1024,128]{2,1,0:T(8,128)(2,1)S(1)} %copy-done.28), channel_id=1, source_target_pairs={{0,8},{8,0},{16,24},{24,16},{1,9},{9,1},{17,25},{25,17},{2,10},{10... | collective-permute-start | bytes 2359304 | tf_op jit(solution)/shard_map/ppermute | solution.py:19
  430.2 6.5 %collective-permute-start.47 = (bf16[128,256]{1,0:T(8,128)(2,1)S(1)}, bf16[128,256]{1,0:T(8,128)(2,1)S(1)}, u32[]{:S(2)}, u32[]{:S(2)}) collective-permute-start(bf16[128,256]{1,0:T(8,128)(2,1)S(1)} %get-tuple-element.149), channel_id=1, source_target_pairs={{0,2},{2,0},{4,6},{6,4},{1,3},{3,1},{5,7},{7,5},{8,10},{10,8},{12,... | collective-permute-start | bytes 196616 | tf_op jit(solution)/shard_map/ppermute | solution.py:19
  434.2 8.0 %collective-permute-start.48 = (bf16[128,256]{1,0:T(8,128)(2,1)S(1)}, bf16[128,256]{1,0:T(8,128)(2,1)S(1)}, u32[]{:S(2)}, u32[]{:S(2)}) collective-permute-start(bf16[128,256]{1,0:T(8,128)(2,1)S(1)} %get-tuple-element.151), channel_id=1, source_target_pairs={{0,4},{2,6},{4,0},{6,2},{1,5},{3,7},{5,1},{7,3},{8,12},{10,14},{12... | collective-permute-start | bytes 196616 | tf_op jit(solution)/shard_map/ppermute | solution.py:19
  434.7 9.5 %collective-permute-start.49 = (bf16[128,256]{1,0:T(8,128)(2,1)S(1)}, bf16[128,256]{1,0:T(8,128)(2,1)S(1)}, u32[]{:S(2)}, u32[]{:S(2)}) collective-permute-start(bf16[128,256]{1,0:T(8,128)(2,1)S(1)} %get-tuple-element.150), channel_id=1, source_target_pairs={{0,6},{2,4},{4,2},{6,0},{1,7},{3,5},{5,3},{7,1},{8,14},{10,12},{12... | collective-permute-start | bytes 196616 | tf_op jit(solution)/shard_map/ppermute | solution.py:19
  436.7 38.8 %collective-permute-start.32 = (bf16[3,1024,128]{2,1,0:T(8,128)(2,1)S(1)}, bf16[3,1024,128]{2,1,0:T(8,128)(2,1)S(1)}, u32[]{:S(2)}, u32[]{:S(2)}) collective-permute-start(bf16[3,1024,128]{2,1,0:T(8,128)(2,1)S(1)} %copy-done.27), channel_id=1, source_target_pairs={{0,16},{8,24},{16,0},{24,8},{1,17},{9,25},{17,1},{25,9},{2,18},{10... | collective-permute-start | bytes 2359304 | tf_op jit(solution)/shard_map/ppermute | solution.py:19
  442.3 33.3 %collective-permute-start.33 = (bf16[3,1024,128]{2,1,0:T(8,128)(2,1)S(1)}, bf16[3,1024,128]{2,1,0:T(8,128)(2,1)S(1)}, u32[]{:S(2)}, u32[]{:S(2)}) collective-permute-start(bf16[3,1024,128]{2,1,0:T(8,128)(2,1)S(1)} %copy-done.26), channel_id=1, source_target_pairs={{0,24},{8,16},{16,8},{24,0},{1,25},{9,17},{17,9},{25,1},{2,26},{10... | collective-permute-start | bytes 2359304 | tf_op jit(solution)/shard_map/ppermute | solution.py:19
  444.2 19.3 %collective-permute-start.50 = (bf16[128,256]{1,0:T(8,128)(2,1)S(1)}, bf16[128,256]{1,0:T(8,128)(2,1)S(1)}, u32[]{:S(2)}, u32[]{:S(2)}) collective-permute-start(bf16[128,256]{1,0:T(8,128)(2,1)S(1)} %add_convert_fusion.9), channel_id=1, source_target_pairs={{0,8},{8,0},{16,24},{24,16},{1,9},{9,1},{17,25},{25,17},{2,10},{10... | collective-permute-start | bytes 196616 | tf_op jit(solution)/shard_map/ppermute | solution.py:19
  468.7 6.7 %collective-permute-start.52 = (bf16[128,256]{1,0:T(8,128)(2,1)S(1)}, bf16[128,256]{1,0:T(8,128)(2,1)S(1)}, u32[]{:S(2)}, u32[]{:S(2)}) collective-permute-start(bf16[128,256]{1,0:T(8,128)(2,1)S(1)} %add_convert_fusion.9), channel_id=1, source_target_pairs={{0,16},{8,24},{16,0},{24,8},{1,17},{9,25},{17,1},{25,9},{2,18},{10... | collective-permute-start | bytes 196616 | tf_op jit(solution)/shard_map/ppermute | solution.py:19
  477.2 9.9 %collective-permute-start.34 = (bf16[3,256,128]{2,1,0:T(8,128)(2,1)S(1)}, bf16[3,256,128]{2,1,0:T(8,128)(2,1)S(1)}, u32[]{:S(2)}, u32[]{:S(2)}) collective-permute-start(bf16[3,256,128]{2,1,0:T(8,128)(2,1)S(1)} %get-tuple-element.138), channel_id=1, source_target_pairs={{0,2},{2,0},{4,6},{6,4},{1,3},{3,1},{5,7},{7,5},{8,10},{10,8},{12,... | collective-permute-start | bytes 589832 | tf_op jit(solution)/shard_map/ppermute | solution.py:19
  478.7 15.5 %collective-permute-start.35 = (bf16[3,256,128]{2,1,0:T(8,128)(2,1)S(1)}, bf16[3,256,128]{2,1,0:T(8,128)(2,1)S(1)}, u32[]{:S(2)}, u32[]{:S(2)}) collective-permute-start(bf16[3,256,128]{2,1,0:T(8,128)(2,1)S(1)} %get-tuple-element.140), channel_id=1, source_target_pairs={{0,4},{2,6},{4,0},{6,2},{1,5},{3,7},{5,1},{7,3},{8,12},{10,14},{12... | collective-permute-start | bytes 589832 | tf_op jit(solution)/shard_map/ppermute | solution.py:19
  479.6 14.6 %collective-permute-start.36 = (bf16[3,256,128]{2,1,0:T(8,128)(2,1)S(1)}, bf16[3,256,128]{2,1,0:T(8,128)(2,1)S(1)}, u32[]{:S(2)}, u32[]{:S(2)}) collective-permute-start(bf16[3,256,128]{2,1,0:T(8,128)(2,1)S(1)} %get-tuple-element.139), channel_id=1, source_target_pairs={{0,6},{2,4},{4,2},{6,0},{1,7},{3,5},{5,3},{7,1},{8,14},{10,12},{12... | collective-permute-start | bytes 589832 | tf_op jit(solution)/shard_map/ppermute | solution.py:19
  496.1 7.2 %collective-permute-start.38 = (bf16[3,256,128]{2,1,0:T(8,128)(2,1)S(1)}, bf16[3,256,128]{2,1,0:T(8,128)(2,1)S(1)}, u32[]{:S(2)}, u32[]{:S(2)}) collective-permute-start(bf16[3,256,128]{2,1,0:T(8,128)(2,1)S(1)} %add_convert_fusion.8), channel_id=1, source_target_pairs={{0,24},{8,16},{16,8},{24,0},{1,25},{9,17},{17,9},{25,1},{2,26},{10... | collective-permute-start | bytes 589832 | tf_op jit(solution)/shard_map/ppermute | solution.py:19
  497.4 7.8 %collective-permute-start.39 = (bf16[3,256,128]{2,1,0:T(8,128)(2,1)S(1)}, bf16[3,256,128]{2,1,0:T(8,128)(2,1)S(1)}, u32[]{:S(2)}, u32[]{:S(2)}) collective-permute-start(bf16[3,256,128]{2,1,0:T(8,128)(2,1)S(1)} %add_convert_fusion.8), channel_id=1, source_target_pairs={{0,16},{8,24},{16,0},{24,8},{1,17},{9,25},{17,1},{25,9},{2,18},{10... | collective-permute-start | bytes 589832 | tf_op jit(solution)/shard_map/ppermute | solution.py:19
  509.8 8.6 %collective-permute-start.40 = (f32[6144]{0:T(1024)S(1)}, f32[6144]{0:T(1024)S(1)}, u32[]{:S(2)}, u32[]{:S(2)}) collective-permute-start(f32[6144]{0:T(1024)S(1)} %pad_maximum_fusion.3), channel_id=1, source_target_pairs={{0,8},{8,0},{16,24},{24,16},{1,9},{9,1},{17,25},{25,17},{2,10},{10... | collective-permute-start | bytes 73736 | tf_op jit(solution)/shard_map/ppermute | solution.py:19
  (79 other events, 938.4 us)
